TPU v7x, 32 devices: a whole 2x2x4 slice. The times are simulated.
32 devices in a mesh: parts: 2 (over x), seq: 16 (over z, y, core).
Axes of the slice: x: 2, y: 2, z: 4, core: 2. Of those that a mesh axis runs over, the one named last changes fastest.
Arguments:
- tokens: bfloat16 [131072, 512], P(('parts', 'seq')), parts along dimension 0, may hold values from -6 to 6
- w_value: bfloat16 [512, 512], replicated, may hold values from -0.25 to 0.25
- w_gate: bfloat16 [512, 512], replicated, may hold values from -0.25 to 0.25
- first_block: bfloat16 [256, 256], replicated, may hold values from -0.375 to 0.375
- second_block: bfloat16 [256, 256], replicated, may hold values from -0.375 to 0.375
- third_block: bfloat16 [256, 256], replicated, may hold values from -0.375 to 0.375
- fourth_block: bfloat16 [256, 256], replicated, may hold values from -0.375 to 0.375
- kernel: bfloat16 [512, 256, 256], P('seq'), may hold values from -6 to 6
- skip_gain: float32 [512], replicated, may hold values from 0.25 to 2
- cotangent: bfloat16 [131072, 512], P(('parts', 'seq')), parts along dimension 0, may hold values from -6 to 6
Outputs:
- grad_tokens: bfloat16 [131072, 512], P(('parts', 'seq')), parts along dimension 0
- grad_kernel: bfloat16 [1024, 256, 256], P(('parts', 'seq')), parts along dimension 0
- grad_weights: float32 [4, 512, 512], P('parts'), parts along dimension 0
- grad_skip: float32 [1024], P('parts'), parts along dimension 0
There are 2 independent parts, one for each index of `parts`. A program takes and returns all parts, laid end to end along the dimension named above; an argument that names none is the same for every part. Nothing has to cross between parts.
All inputs are finite; a program needn't handle non-finite values.
Results may differ from a plain program's by a relative error of at most 0.025.
Values may be sent and summed in bfloat16 or wider, within the bound.
A program may use at most 128 MiB of HBM per device.

v0:
```python
import jax
import jax.numpy as jnp
from jax import lax
from jax.sharding import PartitionSpec as P

D = 512
N1 = 256
N2 = 256


def on_device(
    tokens,
    w_value,
    w_gate,
    first_block,
    second_block,
    third_block,
    fourth_block,
    kernel,
    skip_gain,
    cotangent,
):
    f32 = jnp.float32
    bf16 = jnp.bfloat16
    n_devices = lax.axis_size("seq")
    rows_here = N1 // n_devices
    local_rows = tokens.shape[0]
    value = jnp.dot(tokens, w_value, preferred_element_type=f32).astype(bf16)
    gate = jnp.dot(tokens, w_gate, preferred_element_type=f32).astype(bf16)
    cube = value.reshape(rows_here, N2, D)
    section_one = jnp.einsum("abc,pb->cap", cube, first_block, preferred_element_type=f32).astype(
        bf16
    )
    spectrum = jnp.einsum(
        "cap,qa->cqp",
        lax.all_to_all(section_one, "seq", split_axis=0, concat_axis=1, tiled=True),
        second_block,
        preferred_element_type=f32,
    )
    filtered = (spectrum * kernel.astype(f32)).astype(bf16)
    section_three = jnp.einsum(
        "cqp,rq->crp", filtered, third_block, preferred_element_type=f32
    ).astype(bf16)
    split_three = section_three.reshape(section_three.shape[0], n_devices, rows_here, N2)
    conv = jnp.einsum(
        "crp,sp->rsc",
        lax.all_to_all(split_three, "seq", split_axis=1, concat_axis=0, tiled=True)[:, 0],
        fourth_block,
        preferred_element_type=f32,
    )
    mixed = conv.reshape(local_rows, D) + skip_gain * value.astype(f32)
    upstream = cotangent.astype(f32)
    d_mix = (upstream * gate.astype(f32)).astype(bf16)
    d_gate = (upstream * mixed).astype(bf16)
    d_mix_cube = d_mix.reshape(rows_here, N2, D)
    d_three = jnp.einsum(
        "rsc,sp->crp", d_mix_cube, fourth_block, preferred_element_type=f32
    ).astype(bf16)
    d_freq = jnp.einsum(
        "crp,rq->cqp",
        lax.all_to_all(d_three, "seq", split_axis=0, concat_axis=1, tiled=True),
        third_block,
        preferred_element_type=f32,
    )
    grad_kernel = (d_freq * spectrum).astype(bf16)
    d_spec = (d_freq * kernel.astype(f32)).astype(bf16)
    d_one = jnp.einsum("cqp,qa->cap", d_spec, second_block, preferred_element_type=f32).astype(bf16)
    split_one = d_one.reshape(d_one.shape[0], n_devices, rows_here, N2)
    d_cube = jnp.einsum(
        "cap,pb->abc",
        lax.all_to_all(split_one, "seq", split_axis=1, concat_axis=0, tiled=True)[:, 0],
        first_block,
        preferred_element_type=f32,
    )
    d_value = (d_cube.reshape(local_rows, D) + skip_gain * d_mix.astype(f32)).astype(bf16)
    grad_tokens = (
        jnp.dot(d_value, w_value.T, preferred_element_type=f32)
        + jnp.dot(d_gate, w_gate.T, preferred_element_type=f32)
    ).astype(bf16)
    factor = 1.0 / jnp.sqrt(jnp.asarray(N1 * N2, f32))
    value_term = jnp.dot(tokens.T, d_value, preferred_element_type=f32) * factor
    gate_term = jnp.dot(tokens.T, d_gate, preferred_element_type=f32) * factor
    skip_term = jnp.sum(d_mix.astype(f32) * value.astype(f32), axis=0) * factor
    value_total, gate_total, skip_total = (
        lax.psum(value_term.astype(jnp.bfloat16), "seq").astype(jnp.float32),
        lax.psum(gate_term.astype(jnp.bfloat16), "seq").astype(jnp.float32),
        lax.psum(skip_term.astype(jnp.bfloat16), "seq").astype(jnp.float32),
    )
    return (grad_tokens, grad_kernel, jnp.stack([value_total, gate_total]), skip_total)


def solution(mesh):
    in_specs = (
        P(("parts", "seq"), None),
        P(),
        P(),
        P(),
        P(),
        P(),
        P(),
        P("seq", None, None),
        P(),
        P(("parts", "seq"), None),
    )
    out_specs = (
        P(("parts", "seq"), None),
        P(("parts", "seq"), None, None),
        P("parts", None, None),
        P("parts"),
    )
    return jax.shard_map(
        on_device, mesh=mesh, in_specs=in_specs, out_specs=out_specs, check_vma=False
    )
```

profile of v0, /device:TPU:25, one launch (start us, length us, event | category | flops | bytes accessed | tf_op | source)
XLA Modules:
  0.0 593.3 jit_solution(15915618487453710336)
XLA Ops:
  7.2 6.0 %fusion = bf16[4096,512]{1,0:T(8,128)(2,1)S(1)} fusion(bf16[4096,512]{1,0:T(8,128)(2,1)} %param.19, bf16[4096,512]{1,0:T(8,128)(2,1)} %param.10, bf16[512,512]{1,0:T(8,128)(2,1)} %param.12), kind=kOutput, calls=%fused_computation.7 | convolution fusion | flops 2157969408 | bytes 13107200 | tf_op jit(solution)/shard_map/dot_general | solution.py:29
  16.5 4.4 copy.60
  20.9 6.4 %all-to-all-start = ((bf16[512,16,256]{2,1,0:T(8,128)(2,1)}), bf16[512,16,256]{2,1,0:T(8,128)(2,1)}, u32[]{:S(2)}, u32[]{:S(2)}) async-start(bf16[512,16,256]{2,1,0:T(8,128)(2,1)} %copy.60), calls=%async_computation | async-start | bytes 8388608 | tf_op jit(solution)/shard_map/all_to_all | solution.py:61
  27.3 4.6 convolution_convert_fusion
  35.2 4.4 copy.70
  39.6 74.2 %all-to-all-done = bf16[512,16,256]{2,1,0:T(8,128)(2,1)} async-done(((bf16[512,16,256]{2,1,0:T(8,128)(2,1)}), bf16[512,16,256]{2,1,0:T(8,128)(2,1)}, u32[]{:S(2)}, u32[]{:S(2)}) %all-to-all-start) | async-done | bytes 4194336 | tf_op jit(solution)/shard_map/all_to_all | solution.py:61
  113.7 10.8 %all-to-all-start.2 = ((bf16[512,16,256]{2,1,0:T(8,128)(2,1)}), bf16[512,16,256]{2,1,0:T(8,128)(2,1)}, u32[]{:S(2)}, u32[]{:S(2)}) async-start(bf16[512,16,256]{2,1,0:T(8,128)(2,1)} %copy.70), calls=%async_computation.2 | async-start | bytes 8388608 | tf_op jit(solution)/shard_map/all_to_all | solution.py:36
  124.5 6.4 %copy.63 = bf16[32,256,256]{1,2,0:T(8,128)(2,1)} copy(bf16[32,256,256]{2,1,0:T(8,128)(2,1)} %param.17) | data formatting | bytes 8388608 | tf_op args[7]
  130.9 4.7 copy.61
  135.6 75.4 %all-to-all-done.2 = bf16[512,16,256]{2,1,0:T(8,128)(2,1)} async-done(((bf16[512,16,256]{2,1,0:T(8,128)(2,1)}), bf16[512,16,256]{2,1,0:T(8,128)(2,1)}, u32[]{:S(2)}, u32[]{:S(2)}) %all-to-all-start.2) | async-done | bytes 4194336 | tf_op jit(solution)/shard_map/all_to_all | solution.py:36
  225.1 10.8 %all-to-all-start.3 = ((bf16[32,16,16,256]{3,2,0,1:T(8,128)(2,1)}), bf16[32,16,16,256]{3,2,0,1:T(8,128)(2,1)}, u32[]{:S(2)}, u32[]{:S(2)}) async-start(bf16[32,16,16,256]{3,2,0,1:T(8,128)(2,1)} %copy.74), calls=%async_computation.3 | async-start | bytes 8388608 | tf_op jit(solution)/shard_map/all_to_all | solution.py:47
  235.9 6.0 %fusion.13 = bf16[32,256,256]{1,2,0:T(8,128)(2,1)S(1)} fusion(bf16[32,256,256]{1,2,0:T(8,128)(2,1)} %copy.63, f32[32,256,256]{2,1,0:T(8,128)} %copy-done.1, bf16[256,256]{1,0:T(8,128)(2,1)S(1)} %copy-done.9), kind=kOutput, calls=%fused_computation.24 | convolution fusion | flops 1082130432 | bytes 16908288 | tf_op jit(solution)/shard_map/cqp,qa->cap/dot_general | solution.py:67
  244.2 78.2 %all-to-all-done.3 = bf16[32,16,16,256]{3,2,0,1:T(8,128)(2,1)} async-done(((bf16[32,16,16,256]{3,2,0,1:T(8,128)(2,1)}), bf16[32,16,16,256]{3,2,0,1:T(8,128)(2,1)}, u32[]{:S(2)}, u32[]{:S(2)}) %all-to-all-start.3) | async-done | bytes 4194336 | tf_op jit(solution)/shard_map/all_to_all | solution.py:47
  322.4 10.8 %all-to-all-start.1 = ((bf16[32,16,16,256]{3,2,0,1:T(8,128)(2,1)}), bf16[32,16,16,256]{3,2,0,1:T(8,128)(2,1)}, u32[]{:S(2)}, u32[]{:S(2)}) async-start(bf16[32,16,16,256]{3,2,0,1:T(8,128)(2,1)} %copy.66), calls=%async_computation.1 | async-start | bytes 8388608 | tf_op jit(solution)/shard_map/all_to_all | solution.py:71
  333.2 6.4 %copy.76 = bf16[32,256,256]{2,1,0:T(8,128)(2,1)} copy(bf16[32,256,256]{1,2,0:T(8,128)(2,1)} %get-tuple-element.25) | data formatting | bytes 8388608
  343.3 4.5 fusion.32
  347.8 71.8 %all-to-all-done.1 = bf16[32,16,16,256]{3,2,0,1:T(8,128)(2,1)} async-done(((bf16[32,16,16,256]{3,2,0,1:T(8,128)(2,1)}), bf16[32,16,16,256]{3,2,0,1:T(8,128)(2,1)}, u32[]{:S(2)}, u32[]{:S(2)}) %all-to-all-start.1) | async-done | bytes 4194336 | tf_op jit(solution)/shard_map/all_to_all | solution.py:71
  423.5 4.5 fusion.24
  428.0 10.9 %fusion.7 = (f32[512]{0:T(512)S(1)}, bf16[4096,512]{1,0:T(8,128)(2,1)}, bf16[4096,512]{1,0:T(8,128)(2,1)S(1)}) fusion(bf16[4096,512]{1,0:T(8,128)(2,1)} %copy-done.6, bf16[4096,512]{1,0:T(8,128)(2,1)} %copy-done.5, f32[512]{0:T(512)S(1)} %copy-done.13, f32[512,16,256]{0,2,1:T(8,128)} %fusion.24, f32[512,16,256]{0,2,1:T(8,128)S(1)} %bitcast.101, ...), kind=kLoop, calls=%fused_computation.14 | loop fusion | flops 25165312 | bytes 37752832 | tf_op jit(solution)/shard_map/reduce_sum | solution.py:83
  438.8 8.2 %fusion.22 = bf16[1,512,512]{1,2,0:T(8,128)(2,1)} fusion(bf16[4096,512]{1,0:T(8,128)(2,1)} %get-tuple-element.23, bf16[4096,512]{1,0:T(8,128)(2,1)} %param.10), kind=kOutput, calls=%fused_computation.31 | convolution fusion | flops 2148007936 | bytes 8912896 | tf_op jit(solution)/shard_map/dot_general | solution.py:81
  447.0 5.9 fusion.35
  456.1 30.5 %psum.23 = bf16[512]{0:T(512)(128)(2,1)S(1)} all-reduce(bf16[512]{0:T(512)(128)(2,1)S(1)} %multiply_convert_fusion), channel_id=1, replica_groups=mesh['parts'=2,'seq'=16] {'seq'}, use_global_device_ids=true, to_apply=%region_3.0 | all-reduce | flops 512 | bytes 2048 | tf_op jit(solution)/shard_map/psum | solution.py:87
  487.2 9.1 %add_convert_fusion = bf16[4096,512]{1,0:T(8,128)(2,1)} fusion(f32[4096,512]{1,0:T(8,128)} %fusion.35, bf16[4096,512]{1,0:T(8,128)(2,1)} %copy-done.3, bf16[512,512]{1,0:T(8,128)(2,1)S(1)} %copy-done.12), kind=kOutput, calls=%fused_computation.17 | convolution fusion | flops 2151677952 | bytes 17301504 | tf_op jit(solution)/shard_map/dot_general | solution.py:78
  496.3 87.1 %all-reduce.3.cloned.1.call-done = (bf16[1,512,512]{1,2,0:T(8,128)(2,1)}, bf16[1,512,512]{1,2,0:T(8,128)(2,1)}) async-done(((bf16[1,512,512]{1,2,0:T(8,128)(2,1)}, bf16[1,512,512]{1,2,0:T(8,128)(2,1)}), (bf16[1,512,512]{1,2,0:T(8,128)(2,1)}, bf16[1,512,512]{1,2,0:T(8,128)(2,1)})) %all-reduce.3.cloned.1.call-update) | async-done | bytes 1048592 | tf_op jit(solution)/shard_map/psum | solution.py:86
  (52 shorter events, 37.5 us)
Async XLA Ops:
  7.2 20.1 %copy-start = (bf16[512,512]{1,0:T(8,128)(2,1)S(1)}, bf16[512,512]{1,0:T(8,128)(2,1)}, u32[]{:S(2)}) copy-start(bf16[512,512]{1,0:T(8,128)(2,1)} %param.11) | copy-start | bytes 1572868
  7.2 8.0 %copy-start.10 = (bf16[256,256]{1,0:T(8,128)(2,1)S(1)}, bf16[256,256]{1,0:T(8,128)(2,1)}, u32[]{:S(2)}) copy-start(bf16[256,256]{1,0:T(8,128)(2,1)} %param.16) | copy-start | bytes 393220
  13.2 1.9 copy-start.5
  20.9 92.8 %all-to-all-start = ((bf16[512,16,256]{2,1,0:T(8,128)(2,1)}), bf16[512,16,256]{2,1,0:T(8,128)(2,1)}, u32[]{:S(2)}, u32[]{:S(2)}) async-start(bf16[512,16,256]{2,1,0:T(8,128)(2,1)} %copy.60), calls=%async_computation | async-start | bytes 8388608 | tf_op jit(solution)/shard_map/all_to_all | solution.py:61
  27.3 6.6 %copy-start.11 = (bf16[256,256]{1,0:T(8,128)(2,1)S(1)}, bf16[256,256]{1,0:T(8,128)(2,1)}, u32[]{:S(2)}) copy-start(bf16[256,256]{1,0:T(8,128)(2,1)} %param.13) | copy-start | bytes 393220
  31.9 2.0 copy-start.6
  113.7 97.2 %all-to-all-start.2 = ((bf16[512,16,256]{2,1,0:T(8,128)(2,1)}), bf16[512,16,256]{2,1,0:T(8,128)(2,1)}, u32[]{:S(2)}, u32[]{:S(2)}) async-start(bf16[512,16,256]{2,1,0:T(8,128)(2,1)} %copy.70), calls=%async_computation.2 | async-start | bytes 8388608 | tf_op jit(solution)/shard_map/all_to_all | solution.py:36
  211.0 3.4 copy-start.7
  211.0 3.5 copy-start.8
  214.4 1.3 copy-start.9
  215.8 5.6 copy-start.1
  215.8 5.6 copy-start.2
  225.1 97.2 %all-to-all-start.3 = ((bf16[32,16,16,256]{3,2,0,1:T(8,128)(2,1)}), bf16[32,16,16,256]{3,2,0,1:T(8,128)(2,1)}, u32[]{:S(2)}, u32[]{:S(2)}) async-start(bf16[32,16,16,256]{3,2,0,1:T(8,128)(2,1)} %copy.74), calls=%async_computation.3 | async-start | bytes 8388608 | tf_op jit(solution)/shard_map/all_to_all | solution.py:47
  322.4 97.2 %all-to-all-start.1 = ((bf16[32,16,16,256]{3,2,0,1:T(8,128)(2,1)}), bf16[32,16,16,256]{3,2,0,1:T(8,128)(2,1)}, u32[]{:S(2)}, u32[]{:S(2)}) async-start(bf16[32,16,16,256]{3,2,0,1:T(8,128)(2,1)} %copy.66), calls=%async_computation.1 | async-start | bytes 8388608 | tf_op jit(solution)/shard_map/all_to_all | solution.py:71
  333.2 250.2 %all-reduce.3.cloned.1.call-start = ((), (), s32[]{:S(2)}) async-start(), calls=%async_computation.4 | async-start | bytes 2097152 | tf_op jit(solution)/shard_map/psum | solution.py:86
  419.6 8.3 %slice-start = ((s8[8388608]{0:T(1024)(128)(4,1)}), s8[4194304]{0:T(1024)(128)(4,1)S(1)}, s32[]{:S(2)}) async-start(s8[8388608]{0:T(1024)(128)(4,1)} %bitcast.100), calls=%async_computation.5 | async-start | bytes 8388608
  423.4 4.5 slice-start.1
  423.4 4.5 copy-start.13
  438.8 14.1 %copy-start.3 = (bf16[4096,512]{1,0:T(8,128)(2,1)}, bf16[4096,512]{1,0:T(8,128)(2,1)S(1)}, u32[]{:S(2)}) copy-start(bf16[4096,512]{1,0:T(8,128)(2,1)S(1)} %get-tuple-element.24) | copy-start | bytes 12582916
  438.8 8.2 %copy-start.4 = (bf16[4096,512]{1,0:T(8,128)(2,1)S(1)}, bf16[4096,512]{1,0:T(8,128)(2,1)}, u32[]{:S(2)}) copy-start(bf16[4096,512]{1,0:T(8,128)(2,1)} %get-tuple-element.23) | copy-start | bytes 12582916
  447.0 5.9 copy-start.14
  452.9 34.3 %copy-start.12 = (bf16[512,512]{1,0:T(8,128)(2,1)S(1)}, bf16[512,512]{1,0:T(8,128)(2,1)}, u32[]{:S(2)}) copy-start(bf16[512,512]{1,0:T(8,128)(2,1)} %param.12) | copy-start | bytes 1572868
Sparse Core Ops, SparseCore 0:
  487.3 95.9 all-reduce.2
where the time goes:
time: 599 us; the launch traced here: 593 us
  waiting for transfers between devices  387 us (65%)
  matrix products  60.4 us (10%)
  local copies, waits for them, and re-layouts  50.1 us (8%)
  starting transfers between devices  38.8 us (6%)
  blocking collectives  30.5 us (5%)
  between operations  14.2 us (2%)
  other arithmetic  12.8 us (2%)
    psum x1, waiting for transfers between devices, on_device(): lax.psum(gate_term.astype(jnp.bfloat16), 'seq').astype(jnp.float32)  87.1 us
    all_to_all x1, waiting for transfers between devices, on_device(): lax.all_to_all(split_three, 'seq', split_axis=1, concat_axis=0, tiled=True)  78.2 us
    all_to_all x1, waiting for transfers between devices, on_device(): lax.all_to_all(section_one, 'seq', split_axis=0, concat_axis=1, tiled=True)  75.4 us
    all_to_all x1, waiting for transfers between devices, on_device(): lax.all_to_all(d_three, 'seq', split_axis=0, concat_axis=1, tiled=True)  74.2 us
    all_to_all x1, waiting for transfers between devices, on_device(): lax.all_to_all(split_one, 'seq', split_axis=1, concat_axis=0, tiled=True)  71.8 us
    psum x1, blocking collectives, on_device(): lax.psum(skip_term.astype(jnp.bfloat16), 'seq').astype(jnp.float32)  30.5 us
    unnamed x37, local copies, waits for them, and re-layouts  21.5 us
  transfers between devices with their start and end apart: 5, of which 5 were waited for; matrix products, arithmetic and copies ran while one was open for 9% of the time, Pallas kernels for 0%

commit v1 on v0

v1 whole, which is shorter than its diff:
```python
import functools

import jax
import jax.numpy as jnp
from jax import lax
from jax.experimental import pallas as pl
from jax.experimental.pallas import tpu as pltpu
from jax.sharding import PartitionSpec as P

MESH = pl.DeviceIdType.MESH
f32 = jnp.float32
bf16 = jnp.bfloat16


def reduce_kernel(n, x_ref, s_ref, out_ref, skip_ref, pair, mine, slots, skips, rs_send, rs_recv, ag_send, ag_recv, sk_send, sk_recv, ps_send, ps_recv):
    me = lax.axis_index("seq")
    core = lax.rem(me, 2)
    chip = lax.div(me, 2)
    chips = n // 2
    partner = me + 1 - 2 * core
    rows = x_ref.shape[0]
    half = rows // 2
    part = half // chips

    barrier = pltpu.get_barrier_semaphore()

    def greet(k, carry):
        peer = lax.rem(me + k, n)
        pl.semaphore_signal(barrier, inc=1, device_id={"seq": peer}, device_id_type=MESH)
        return carry

    lax.fori_loop(1, n, greet, 0)
    pl.semaphore_wait(barrier, n - 1)

    other_half = pl.ds(pl.multiple_of((1 - core) * half, half), half)
    first = pltpu.make_async_remote_copy(
        src_ref=x_ref.at[other_half], dst_ref=pair, send_sem=ps_send, recv_sem=ps_recv,
        device_id={"seq": partner}, device_id_type=MESH)
    first.start()

    def skip_copy(k):
        peer = lax.rem(me + k, n)
        return pltpu.make_async_remote_copy(
            src_ref=s_ref, dst_ref=skips.at[k], send_sem=sk_send.at[k], recv_sem=sk_recv.at[k],
            device_id={"seq": peer}, device_id_type=MESH)

    lax.fori_loop(1, n, lambda k, c: (skip_copy(k).start(), c)[1], 0)
    first.wait()
    my_half = pl.ds(pl.multiple_of(core * half, half), half)
    mine[...] = (x_ref[my_half, :].astype(f32) + pair[...].astype(f32)).astype(bf16)

    def rs_copy(k):
        peer_chip = lax.rem(chip + k, chips)
        src = pl.ds(pl.multiple_of(peer_chip * part, part), part)
        return pltpu.make_async_remote_copy(
            src_ref=mine.at[src], dst_ref=slots.at[k], send_sem=rs_send.at[k], recv_sem=rs_recv.at[k],
            device_id={"seq": 2 * peer_chip + core}, device_id_type=MESH)

    lax.fori_loop(1, chips, lambda k, c: (rs_copy(k).start(), c)[1], 0)
    own = pl.ds(pl.multiple_of(chip * part, part), part)

    def rs_add(k, total):
        rs_copy(k).wait_recv()
        return total + slots[k].astype(f32)

    total = lax.fori_loop(1, chips, rs_add, mine[own, :].astype(f32))
    lax.fori_loop(1, chips, lambda k, c: (rs_copy(k).wait_send(), c)[1], 0)
    place = pl.ds(pl.multiple_of(core * half + chip * part, part), part)
    out_ref[place, :] = total.astype(bf16)

    def ag_copy(k):
        peer = lax.rem(me + k, n)
        return pltpu.make_async_remote_copy(
            src_ref=out_ref.at[place], dst_ref=out_ref.at[place], send_sem=ag_send.at[k], recv_sem=ag_recv.at[k],
            device_id={"seq": peer}, device_id_type=MESH)

    lax.fori_loop(1, n, lambda k, c: (ag_copy(k).start(), c)[1], 0)

    skips[0] = s_ref[...]
    lax.fori_loop(1, n, lambda k, c: (skip_copy(k).wait(), c)[1], 0)

    def skip_add(d, total):
        return total + skips[lax.rem(me - d + n, n)]

    skip_ref[...] = lax.fori_loop(0, n, skip_add, jnp.zeros(s_ref.shape, f32))

    def ag_wait(k, carry):
        ag_copy(k).wait_send()
        ag_copy(k).wait_recv()
        return carry

    lax.fori_loop(1, n, ag_wait, 0)


def all_sum(x, s, n):
    rows, cols = x.shape
    half = rows // 2
    chips = n // 2
    dma = pltpu.SemaphoreType.DMA
    return pl.pallas_call(
        functools.partial(reduce_kernel, n),
        out_shape=(jax.ShapeDtypeStruct(x.shape, bf16), jax.ShapeDtypeStruct(s.shape, f32)),
        in_specs=[pl.BlockSpec(memory_space=pltpu.VMEM)] * 2,
        out_specs=(pl.BlockSpec(memory_space=pltpu.VMEM),) * 2,
        scratch_shapes=[
            pltpu.VMEM((half, cols), bf16),
            pltpu.VMEM((half, cols), bf16),
            pltpu.VMEM((chips, half // chips, cols), bf16),
            pltpu.VMEM((n,) + s.shape, f32),
            dma((chips,)), dma((chips,)), dma((n,)), dma((n,)), dma((n,)), dma((n,)), dma, dma,
        ],
        compiler_params=pltpu.CompilerParams(collective_id=0, has_side_effects=True),
        name="all_sum",
    )(x, s)


def on_device(tokens, w_value, w_gate, first_block, second_block, third_block, fourth_block, kernel, skip_gain, cotangent):
    n = lax.axis_size("seq")
    n1 = second_block.shape[0]
    n2 = first_block.shape[0]
    local_rows, d = tokens.shape
    rows_here = n1 // n
    value = jnp.dot(tokens, w_value, preferred_element_type=f32).astype(bf16)
    cube = value.reshape(rows_here, n2, d)
    section_one = jnp.einsum("abc,pb->cap", cube, first_block, preferred_element_type=f32).astype(bf16)
    one_here = lax.all_to_all(section_one, "seq", split_axis=0, concat_axis=1, tiled=True)

    gate = jnp.dot(tokens, w_gate, preferred_element_type=f32).astype(bf16)
    upstream = cotangent.astype(f32)
    d_mix = (upstream * gate.astype(f32)).astype(bf16)
    d_mix_cube = d_mix.reshape(rows_here, n2, d)
    d_three = jnp.einsum("rsc,sp->crp", d_mix_cube, fourth_block, preferred_element_type=f32).astype(bf16)
    skip_term = jnp.sum(d_mix.astype(f32) * value.astype(f32), axis=0)
    one_here, d_three, skip_term = lax.optimization_barrier((one_here, d_three, skip_term))
    three_here = lax.all_to_all(d_three, "seq", split_axis=0, concat_axis=1, tiled=True)

    spectrum = jnp.einsum("cap,qa->cqp", one_here, second_block, preferred_element_type=f32)
    filtered = (spectrum * kernel.astype(f32)).astype(bf16)
    section_three = jnp.einsum("cqp,rq->crp", filtered, third_block, preferred_element_type=f32).astype(bf16)
    split_three = section_three.reshape(section_three.shape[0], n, rows_here, n2)
    three_here, split_three, spectrum = lax.optimization_barrier((three_here, split_three, spectrum))
    back_three = lax.all_to_all(split_three, "seq", split_axis=1, concat_axis=0, tiled=True)[:, 0]

    d_freq = jnp.einsum("crp,rq->cqp", three_here, third_block, preferred_element_type=f32)
    grad_kernel = (d_freq * spectrum).astype(bf16)
    d_spec = (d_freq * kernel.astype(f32)).astype(bf16)
    d_one = jnp.einsum("cqp,qa->cap", d_spec, second_block, preferred_element_type=f32).astype(bf16)
    split_one = d_one.reshape(d_one.shape[0], n, rows_here, n2)
    back_three, split_one, grad_kernel = lax.optimization_barrier((back_three, split_one, grad_kernel))
    back_one = lax.all_to_all(split_one, "seq", split_axis=1, concat_axis=0, tiled=True)[:, 0]

    conv = jnp.einsum("crp,sp->rsc", back_three, fourth_block, preferred_element_type=f32)
    mixed = conv.reshape(local_rows, d) + skip_gain * value.astype(f32)
    d_gate = (upstream * mixed).astype(bf16)
    factor = 1.0 / jnp.sqrt(jnp.asarray(n1 * n2, f32))
    gate_term = (jnp.dot(tokens.T, d_gate, preferred_element_type=f32) * factor).astype(bf16)
    gate_grad = jnp.dot(d_gate, w_gate.T, preferred_element_type=f32)
    back_one, gate_term, gate_grad = lax.optimization_barrier((back_one, gate_term, gate_grad))

    d_cube = jnp.einsum("cap,pb->abc", back_one, first_block, preferred_element_type=f32)
    d_value = (d_cube.reshape(local_rows, d) + skip_gain * d_mix.astype(f32)).astype(bf16)
    grad_tokens = (jnp.dot(d_value, w_value.T, preferred_element_type=f32) + gate_grad).astype(bf16)
    value_term = (jnp.dot(tokens.T, d_value, preferred_element_type=f32) * factor).astype(bf16)
    skip_rows = jnp.pad((skip_term * factor).reshape(-1, 128), ((0, 8 - d // 128), (0, 0)))
    sums, skip_sum = all_sum(jnp.concatenate([value_term, gate_term]), skip_rows, n)
    return (grad_tokens, grad_kernel, sums.astype(f32).reshape(2, d, d), skip_sum[: d // 128].reshape(d))


def solution(mesh):
    in_specs = (
        P(("parts", "seq"), None), P(), P(), P(), P(), P(), P(), P("seq", None, None), P(), P(("parts", "seq"), None),
    )
    out_specs = (
        P(("parts", "seq"), None), P(("parts", "seq"), None, None), P("parts", None, None), P("parts"),
    )
    return jax.shard_map(on_device, mesh=mesh, in_specs=in_specs, out_specs=out_specs, check_vma=False)
```

time: 599 us -> 508 us (0.85)
  waiting for transfers between devices: 387 us -> 280 us
  Pallas kernels: 0 us -> 48.4 us
  blocking collectives: 30.5 us -> 0 us
  between operations: 14.2 us -> 1.31 us
  matrix products: 60.4 us -> 68.6 us
    psum x1 -> x0, waiting for transfers between devices: 87.1 us -> none  [on_device(): lax.psum(gate_term.astype(jnp.bfloat16), 'seq').astype(jnp.float32)]
    pallas_call x0 -> x1, Pallas kernels: none -> 48.4 us  [all_sum(): pl.pallas_call(functools.partial(reduce_kernel, n), out_shape=(jax.ShapeD...]
    psum x1 -> x0, blocking collectives: 30.5 us -> none  [on_device(): lax.psum(skip_term.astype(jnp.bfloat16), 'seq').astype(jnp.float32)]
    all_to_all x1, waiting for transfers between devices: 71.8 us -> 54.8 us  [on_device(): lax.all_to_all(split_one, 'seq', split_axis=1, concat_axis=0, tiled=True)]
    convert_element_type x2, other arithmetic: 0.59 us -> 14.1 us  [the longest x1 7.78 us: on_device(): d_gate = (upstream * mixed).astype(bf16)]
    optimization_barrier x0 -> x3, local copies, waits for them, and re-layouts: none -> 11.5 us  [the longest x1 4.59 us: on_device(): lax.optimization_barrier((back_three, split_one, grad_kernel))]
    reduce_sum x1 -> x0, other arithmetic: 10.9 us -> none  [on_device(): skip_term = jnp.sum(d_mix.astype(f32) * value.astype(f32), axis=0) * factor]
    all_to_all x2 -> x0, local copies, waits for them, and re-layouts: 7.47 us -> none  [the longest x1 3.81 us: on_device(): lax.all_to_all(split_one, 'seq', split_axis=1, concat_axis=0, tiled=True)]
  transfers between devices with their start and end apart: 5 -> 4, of which waited for: 5 -> 4; matrix products, arithmetic and copies ran while one was open for 9% -> 12% of each run, Pallas kernels for 0% -> 0%
where the time goes in v1:
time: 508 us; the launch traced here: 500 us
  waiting for transfers between devices  280 us (55%)
  matrix products  68.6 us (14%)
  Pallas kernels  48.4 us (10%)
  local copies, waits for them, and re-layouts  44.8 us (9%)
  starting transfers between devices  39.2 us (8%)
  other arithmetic  17.9 us (4%)
    all_to_all x1, waiting for transfers between devices, on_device(): lax.all_to_all(section_one, 'seq', split_axis=0, concat_axis=1, tiled=True)  80.7 us
    all_to_all x1, waiting for transfers between devices, on_device(): lax.all_to_all(split_three, 'seq', split_axis=1, concat_axis=0, tiled=True)  74.9 us
    all_to_all x1, waiting for transfers between devices, on_device(): lax.all_to_all(d_three, 'seq', split_axis=0, concat_axis=1, tiled=True)  69.7 us
    all_to_all x1, waiting for transfers between devices, on_device(): lax.all_to_all(split_one, 'seq', split_axis=1, concat_axis=0, tiled=True)  54.8 us
    pallas_call x1, Pallas kernels, all_sum(): pl.pallas_call(functools.partial(reduce_kernel, n), out_shape=(jax.ShapeD...  48.4 us
    unnamed x38, local copies, waits for them, and re-layouts  17.1 us
    all_to_all x1, starting transfers between devices, on_device(): lax.all_to_all(split_one, 'seq', split_axis=1, concat_axis=0, tiled=True)  10.8 us
    all_to_all x1, starting transfers between devices, on_device(): lax.all_to_all(split_three, 'seq', split_axis=1, concat_axis=0, tiled=True)  10.8 us
  transfers between devices with their start and end apart: 4, of which 4 were waited for; matrix products, arithmetic and copies ran while one was open for 12% of the time, Pallas kernels for 0%

profile of v1, /device:TPU:25, one launch (start us, length us, event | category | flops | bytes accessed | tf_op | source)
XLA Modules:
  0.0 500.4 jit_solution(3742322540770199928)
XLA Ops:
  0.7 6.1 %fusion = bf16[4096,512]{1,0:T(8,128)(2,1)S(1)} fusion(bf16[4096,512]{1,0:T(8,128)(2,1)} %param.19, bf16[4096,512]{1,0:T(8,128)(2,1)} %param.10, bf16[512,512]{1,0:T(8,128)(2,1)} %param.12), kind=kOutput, calls=%fused_computation.7 | convolution fusion | flops 2157969408 | bytes 13107200 | tf_op jit(solution)/shard_map/dot_general | solution.py:128
  15.9 6.8 %all-to-all-start = ((bf16[512,16,256]{2,1,0:T(8,128)(2,1)}), bf16[512,16,256]{2,1,0:T(8,128)(2,1)}, u32[]{:S(2)}, u32[]{:S(2)}) async-start(bf16[512,16,256]{2,1,0:T(8,128)(2,1)} %copy.60), calls=%async_computation | async-start | bytes 8388608 | tf_op jit(solution)/shard_map/all_to_all | solution.py:126
  22.7 5.5 %convert_bitcast_fusion = bf16[512,16,256]{2,0,1:T(8,128)(2,1)} fusion(bf16[16,256,512]{2,1,0:T(8,128)(2,1)} %bitcast.100, bf16[256,256]{1,0:T(8,128)(2,1)S(1)} %copy-done.10), kind=kOutput, calls=%fused_computation.26 | convolution fusion | flops 1075838976 | bytes 8519680 | tf_op jit(solution)/shard_map/rsc,sp->crp/dot_general | solution.py:132
  28.2 80.7 %all-to-all-done = bf16[512,16,256]{2,1,0:T(8,128)(2,1)} async-done(((bf16[512,16,256]{2,1,0:T(8,128)(2,1)}), bf16[512,16,256]{2,1,0:T(8,128)(2,1)}, u32[]{:S(2)}, u32[]{:S(2)}) %all-to-all-start) | async-done | bytes 4194336 | tf_op jit(solution)/shard_map/all_to_all | solution.py:126
  109.0 4.9 copy.61
  113.9 4.5 copy.63
  118.3 10.8 %all-to-all-start.1 = ((bf16[512,16,256]{2,1,0:T(8,128)(2,1)}), bf16[512,16,256]{2,1,0:T(8,128)(2,1)}, u32[]{:S(2)}, u32[]{:S(2)}) async-start(bf16[512,16,256]{2,1,0:T(8,128)(2,1)} %copy.63), calls=%async_computation.1 | async-start | bytes 8388608 | tf_op jit(solution)/shard_map/all_to_all | solution.py:135
  129.1 6.5 %copy.66 = bf16[32,256,256]{1,2,0:T(8,128)(2,1)} copy(bf16[32,256,256]{2,1,0:T(8,128)(2,1)} %param.17) | data formatting | bytes 8388608 | tf_op args[7]
  145.9 69.7 %all-to-all-done.1 = bf16[512,16,256]{2,1,0:T(8,128)(2,1)} async-done(((bf16[512,16,256]{2,1,0:T(8,128)(2,1)}), bf16[512,16,256]{2,1,0:T(8,128)(2,1)}, u32[]{:S(2)}, u32[]{:S(2)}) %all-to-all-start.1) | async-done | bytes 4194336 | tf_op jit(solution)/shard_map/all_to_all | solution.py:135
  215.6 4.9 copy.64
  223.0 10.8 %all-to-all-start.2 = ((bf16[32,16,16,256]{3,2,0,1:T(8,128)(2,1)}), bf16[32,16,16,256]{3,2,0,1:T(8,128)(2,1)}, u32[]{:S(2)}, u32[]{:S(2)}) async-start(bf16[32,16,16,256]{3,2,0,1:T(8,128)(2,1)} %copy.68), calls=%async_computation.2 | async-start | bytes 8388608 | tf_op jit(solution)/shard_map/all_to_all | solution.py:142
  233.8 8.1 %fusion.8 = (bf16[32,256,256]{1,2,0:T(8,128)(2,1)}, f32[32,256,256]{2,1,0:T(8,128)S(1)}) fusion(f32[32,256,256]{1,2,0:T(8,128)} %copy-done.1, bf16[32,256,256]{2,1,0:T(8,128)(2,1)} %bitcast.103, bf16[256,256]{1,0:T(8,128)(2,1)S(1)} %copy-done.8), kind=kOutput, calls=%fused_computation.16 | convolution fusion | flops 1077936128 | bytes 25296896 | tf_op jit(solution)/shard_map/crp,rq->cqp/dot_general | solution.py:144
  245.3 74.9 %all-to-all-done.2 = bf16[32,16,16,256]{3,2,0,1:T(8,128)(2,1)} async-done(((bf16[32,16,16,256]{3,2,0,1:T(8,128)(2,1)}), bf16[32,16,16,256]{3,2,0,1:T(8,128)(2,1)}, u32[]{:S(2)}, u32[]{:S(2)}) %all-to-all-start.2) | async-done | bytes 4194336 | tf_op jit(solution)/shard_map/all_to_all | solution.py:142
  320.2 4.6 copy.72
  324.8 10.8 %all-to-all-start.3 = ((bf16[32,16,16,256]{3,2,0,1:T(8,128)(2,1)}), bf16[32,16,16,256]{3,2,0,1:T(8,128)(2,1)}, u32[]{:S(2)}, u32[]{:S(2)}) async-start(bf16[32,16,16,256]{3,2,0,1:T(8,128)(2,1)} %copy.72), calls=%async_computation.3 | async-start | bytes 8388608 | tf_op jit(solution)/shard_map/all_to_all | solution.py:150
  336.2 6.6 %copy.77 = bf16[32,256,256]{2,1,0:T(8,128)(2,1)} copy(bf16[32,256,256]{1,2,0:T(8,128)(2,1)} %get-tuple-element.45) | data formatting | bytes 8388608
  342.8 8.5 %fusion.15 = f32[512,16,256]{0,2,1:T(8,128)} fusion(bf16[512,16,256]{2,1,0:T(8,128)(2,1)} %bitcast.19, bf16[256,256]{1,0:T(8,128)(2,1)S(1)} %copy-done.10), kind=kOutput, calls=%fused_computation.24 | convolution fusion | flops 1073741824 | bytes 12713984 | tf_op jit(solution)/shard_map/crp,sp->rsc/dot_general | solution.py:152
  351.3 7.8 %fusion.1 = bf16[4096,512]{1,0:T(8,128)(2,1)S(1)} fusion(bf16[4096,512]{1,0:T(8,128)(2,1)} %param.19, bf16[4096,512]{1,0:T(8,128)(2,1)} %copy-done.6, f32[512,16,256]{0,2,1:T(8,128)} %fusion.15, f32[512]{0:T(512)S(1)} %copy-done.13), kind=kLoop, calls=%fused_computation.8 | loop fusion | flops 12582912 | bytes 20973568 | tf_op jit(solution)/shard_map/convert_element_type | solution.py:154
  359.2 5.7 %fusion.36 = f32[4096,512]{1,0:T(8,128)} fusion(bf16[4096,512]{1,0:T(8,128)(2,1)S(1)} %fusion.1, bf16[512,512]{1,0:T(8,128)(2,1)S(1)} %copy-done.12), kind=kOutput, calls=%fused_computation.49 | convolution fusion | flops 2147483648 | bytes 13107200 | tf_op jit(solution)/shard_map/dot_general | solution.py:157
  367.2 54.8 %all-to-all-done.3 = bf16[32,16,16,256]{3,2,0,1:T(8,128)(2,1)} async-done(((bf16[32,16,16,256]{3,2,0,1:T(8,128)(2,1)}), bf16[32,16,16,256]{3,2,0,1:T(8,128)(2,1)}, u32[]{:S(2)}, u32[]{:S(2)}) %all-to-all-start.3) | async-done | bytes 4194336 | tf_op jit(solution)/shard_map/all_to_all | solution.py:150
  422.0 9.1 %fusion.13 = f32[512,16,256]{0,2,1:T(8,128)} fusion(bf16[512,16,256]{2,1,0:T(8,128)(2,1)} %bitcast.26, bf16[256,256]{1,0:T(8,128)(2,1)S(1)} %copy-done.11), kind=kOutput, calls=%fused_computation.22 | convolution fusion | flops 1073741824 | bytes 12713984 | tf_op jit(solution)/shard_map/cap,pb->abc/dot_general | solution.py:160
  431.1 6.3 %fusion.3 = bf16[4096,512]{1,0:T(8,128)(2,1)S(1)} fusion(bf16[4096,512]{1,0:T(8,128)(2,1)} %copy-done.4, f32[512,16,256]{0,2,1:T(8,128)} %fusion.13, f32[512]{0:T(512)S(1)} %copy-done.13), kind=kLoop, calls=%fused_computation.10 | loop fusion | flops 8388608 | bytes 16779264 | tf_op jit(solution)/shard_map/convert_element_type | solution.py:161
  437.4 4.6 fusion.25
  447.4 48.4 %all_sum.1 = (bf16[1024,512]{1,0:T(8,128)(2,1)}, f32[8,128]{1,0:T(8,128)}) custom-call(bf16[1024,512]{1,0:T(8,128)(2,1)} %pad_maximum_fusion.x_ref, f32[8,128]{1,0:T(8,128)} %pad.4.s_ref), custom_call_target="tpu_custom_call" | custom-call | tf_op jit(solution)/shard_map/all_sum/pallas_call | solution.py:100
  (51 shorter events, 37.8 us)
Async XLA Ops:
  0.6 6.1 %copy-start = (bf16[512,512]{1,0:T(8,128)(2,1)S(1)}, bf16[512,512]{1,0:T(8,128)(2,1)}, u32[]{:S(2)}) copy-start(bf16[512,512]{1,0:T(8,128)(2,1)} %param.11) | copy-start | bytes 1572868
  0.6 6.1 %copy-start.14 = (bf16[4096,512]{1,0:T(8,128)(2,1)S(1)}, bf16[4096,512]{1,0:T(8,128)(2,1)}, u32[]{:S(2)}) copy-start(bf16[4096,512]{1,0:T(8,128)(2,1)} %param.10) | copy-start | bytes 12582916
  6.8 2.6 copy-start.4
  6.8 2.6 copy-start.11
  9.4 2.0 copy-start.6
  15.8 6.8 %copy-start.10 = (bf16[256,256]{1,0:T(8,128)(2,1)S(1)}, bf16[256,256]{1,0:T(8,128)(2,1)}, u32[]{:S(2)}) copy-start(bf16[256,256]{1,0:T(8,128)(2,1)} %param.16) | copy-start | bytes 393220
  15.9 93.1 %all-to-all-start = ((bf16[512,16,256]{2,1,0:T(8,128)(2,1)}), bf16[512,16,256]{2,1,0:T(8,128)(2,1)}, u32[]{:S(2)}, u32[]{:S(2)}) async-start(bf16[512,16,256]{2,1,0:T(8,128)(2,1)} %copy.60), calls=%async_computation | async-start | bytes 8388608 | tf_op jit(solution)/shard_map/all_to_all | solution.py:126
  109.0 4.9 copy-start.5
  118.3 97.2 %all-to-all-start.1 = ((bf16[512,16,256]{2,1,0:T(8,128)(2,1)}), bf16[512,16,256]{2,1,0:T(8,128)(2,1)}, u32[]{:S(2)}, u32[]{:S(2)}) async-start(bf16[512,16,256]{2,1,0:T(8,128)(2,1)} %copy.63), calls=%async_computation.1 | async-start | bytes 8388608 | tf_op jit(solution)/shard_map/all_to_all | solution.py:135
  129.1 6.5 %copy-start.9 = (bf16[256,256]{1,0:T(8,128)(2,1)S(1)}, bf16[256,256]{1,0:T(8,128)(2,1)}, u32[]{:S(2)}) copy-start(bf16[256,256]{1,0:T(8,128)(2,1)} %param.14) | copy-start | bytes 393220
  135.6 6.9 %copy-start.2 = (bf16[32,256,256]{1,2,0:T(8,128)(2,1)S(1)}, bf16[32,256,256]{1,2,0:T(8,128)(2,1)}, u32[]{:S(2)}) copy-start(bf16[32,256,256]{1,2,0:T(8,128)(2,1)} %copy.66) | copy-start | bytes 12582916
  135.6 6.9 %copy-start.8 = (bf16[256,256]{1,0:T(8,128)(2,1)S(1)}, bf16[256,256]{1,0:T(8,128)(2,1)}, u32[]{:S(2)}) copy-start(bf16[256,256]{1,0:T(8,128)(2,1)} %param.15) | copy-start | bytes 393220
  139.3 3.3 copy-start.1
  215.6 4.9 copy-start.7
  223.0 97.2 %all-to-all-start.2 = ((bf16[32,16,16,256]{3,2,0,1:T(8,128)(2,1)}), bf16[32,16,16,256]{3,2,0,1:T(8,128)(2,1)}, u32[]{:S(2)}, u32[]{:S(2)}) async-start(bf16[32,16,16,256]{3,2,0,1:T(8,128)(2,1)} %copy.68), calls=%async_computation.2 | async-start | bytes 8388608 | tf_op jit(solution)/shard_map/all_to_all | solution.py:142
  233.8 8.1 %copy-start.3 = (bf16[32,256,256]{1,2,0:T(8,128)(2,1)S(1)}, bf16[32,256,256]{1,2,0:T(8,128)(2,1)}, u32[]{:S(2)}) copy-start(bf16[32,256,256]{1,2,0:T(8,128)(2,1)} %copy.66) | copy-start | bytes 12582916
  324.8 97.2 %all-to-all-start.3 = ((bf16[32,16,16,256]{3,2,0,1:T(8,128)(2,1)}), bf16[32,16,16,256]{3,2,0,1:T(8,128)(2,1)}, u32[]{:S(2)}, u32[]{:S(2)}) async-start(bf16[32,16,16,256]{3,2,0,1:T(8,128)(2,1)} %copy.72), calls=%async_computation.3 | async-start | bytes 8388608 | tf_op jit(solution)/shard_map/all_to_all | solution.py:150
  342.8 8.6 %copy-start.13 = (f32[512]{0:T(512)S(1)}, f32[512]{0:T(512)}, u32[]{:S(2)}) copy-start(f32[512]{0:T(512)} %param.18) | copy-start | bytes 6148
  351.3 7.8 %copy-start.12 = (bf16[512,512]{1,0:T(8,128)(2,1)S(1)}, bf16[512,512]{1,0:T(8,128)(2,1)}, u32[]{:S(2)}) copy-start(bf16[512,512]{1,0:T(8,128)(2,1)} %param.12) | copy-start | bytes 1572868
  359.1 5.7 %copy-start.15 = (bf16[4096,512]{1,0:T(8,128)(2,1)S(1)}, bf16[4096,512]{1,0:T(8,128)(2,1)}, u32[]{:S(2)}) copy-start(bf16[4096,512]{1,0:T(8,128)(2,1)} %param.10) | copy-start | bytes 12582916
  422.0 19.9 %slice-start = ((s8[8388608]{0:T(1024)(128)(4,1)}), s8[4194304]{0:T(1024)(128)(4,1)S(1)}, s32[]{:S(2)}) async-start(s8[8388608]{0:T(1024)(128)(4,1)} %bitcast.98), calls=%async_computation.4 | async-start | bytes 8388608
  431.1 10.9 %slice-start.1 = ((s8[8388608]{0:T(1024)(128)(4,1)}), s8[4194304]{0:T(1024)(128)(4,1)S(1)}, s32[]{:S(2)}) async-start(s8[8388608]{0:T(1024)(128)(4,1)} %bitcast.98), calls=%async_computation.5 | async-start | bytes 8388608

commit v2 on v1

--- a/solution.py
+++ b/solution.py
@@ -12,7 +12,7 @@
 bf16 = jnp.bfloat16
 
 
-def reduce_kernel(n, x_ref, s_ref, out_ref, skip_ref, pair, mine, slots, skips, rs_send, rs_recv, ag_send, ag_recv, sk_send, sk_recv, ps_send, ps_recv):
+def reduce_kernel(n, x_ref, s_ref, out_ref, skip_ref, pair, mine, slots, skips, rs_send, rs_recv, ag_send, ag_recv, fw_send, fw_recv, sk_send, sk_recv, ps_send, ps_recv):
     me = lax.axis_index("seq")
     core = lax.rem(me, 2)
     chip = lax.div(me, 2)
@@ -68,13 +68,23 @@
     place = pl.ds(pl.multiple_of(core * half + chip * part, part), part)
     out_ref[place, :] = total.astype(bf16)
 
+    def rows_of(k):
+        source = lax.rem(chip - k + chips, chips)
+        return pl.ds(pl.multiple_of(core * half + source * part, part), part)
+
     def ag_copy(k):
-        peer = lax.rem(me + k, n)
+        peer_chip = lax.rem(chip + k, chips)
         return pltpu.make_async_remote_copy(
             src_ref=out_ref.at[place], dst_ref=out_ref.at[place], send_sem=ag_send.at[k], recv_sem=ag_recv.at[k],
-            device_id={"seq": peer}, device_id_type=MESH)
-
-    lax.fori_loop(1, n, lambda k, c: (ag_copy(k).start(), c)[1], 0)
+            device_id={"seq": 2 * peer_chip + core}, device_id_type=MESH)
+
+    def pass_on(k):
+        return pltpu.make_async_remote_copy(
+            src_ref=out_ref.at[rows_of(k)], dst_ref=out_ref.at[rows_of(k)], send_sem=fw_send.at[k], recv_sem=fw_recv.at[k],
+            device_id={"seq": partner}, device_id_type=MESH)
+
+    lax.fori_loop(1, chips, lambda k, c: (ag_copy(k).start(), c)[1], 0)
+    pass_on(0).start()
 
     skips[0] = s_ref[...]
     lax.fori_loop(1, n, lambda k, c: (skip_copy(k).wait(), c)[1], 0)
@@ -84,12 +94,14 @@
 
     skip_ref[...] = lax.fori_loop(0, n, skip_add, jnp.zeros(s_ref.shape, f32))
 
-    def ag_wait(k, carry):
-        ag_copy(k).wait_send()
+    def arrived(k, carry):
         ag_copy(k).wait_recv()
-        return carry
-
-    lax.fori_loop(1, n, ag_wait, 0)
+        pass_on(k).start()
+        return carry
+
+    lax.fori_loop(1, chips, arrived, 0)
+    lax.fori_loop(1, chips, lambda k, c: (ag_copy(k).wait_send(), c)[1], 0)
+    lax.fori_loop(0, chips, lambda k, c: (pass_on(k).wait(), c)[1], 0)
 
 
 def all_sum(x, s, n):
@@ -107,11 +119,117 @@
             pltpu.VMEM((half, cols), bf16),
             pltpu.VMEM((chips, half // chips, cols), bf16),
             pltpu.VMEM((n,) + s.shape, f32),
-            dma((chips,)), dma((chips,)), dma((n,)), dma((n,)), dma((n,)), dma((n,)), dma, dma,
+            dma((chips,)), dma((chips,)), dma((chips,)), dma((chips,)), dma((chips,)), dma((chips,)), dma((n,)), dma((n,)), dma, dma,
         ],
         compiler_params=pltpu.CompilerParams(collective_id=0, has_side_effects=True),
         name="all_sum",
     )(x, s)
+
+
+def exchange_kernel(n, one_ref, three_ref, kern_ref, b_ref, bt_ref, g_ref, gt_ref, back3_ref, back1_ref, gk_ref,
+                    held1, held3, spec, s1, r1, s3, r3, sb3, rb3, sb1, rb1, own):
+    me = lax.axis_index("seq")
+    wide = kern_ref.shape[0]
+    rows = one_ref.shape[1]
+    barrier = pltpu.get_barrier_semaphore()
+
+    def greet(k, carry):
+        pl.semaphore_signal(barrier, inc=1, device_id={"seq": lax.rem(me + k, n)}, device_id_type=MESH)
+        return carry
+
+    lax.fori_loop(1, n, greet, 0)
+    pl.semaphore_wait(barrier, n - 1)
+
+    def channels_of(d):
+        return pl.ds(pl.multiple_of(d * wide, wide), wide)
+
+    def rows_of(d):
+        return pl.ds(pl.multiple_of(d * rows, rows), rows)
+
+    def out_copy(src, dst, send, recv, k):
+        peer = lax.rem(me + k, n)
+        return pltpu.make_async_remote_copy(
+            src_ref=src.at[channels_of(peer)], dst_ref=dst.at[:, rows_of(me), :], send_sem=send.at[k], recv_sem=recv.at[k],
+            device_id={"seq": peer}, device_id_type=MESH)
+
+    def back_copy(src, dst, send, recv, k):
+        peer = lax.rem(me + k, n)
+        return pltpu.make_async_remote_copy(
+            src_ref=src.at[:, rows_of(peer), :], dst_ref=dst.at[channels_of(me)], send_sem=send.at[k], recv_sem=recv.at[k],
+            device_id={"seq": peer}, device_id_type=MESH)
+
+    def start_all(copy, *refs):
+        lax.fori_loop(1, n, lambda k, c: (copy(*refs, k).start(), c)[1], 0)
+
+    def wait_all(copy, *refs):
+        lax.fori_loop(1, n, lambda k, c: (copy(*refs, k).wait(), c)[1], 0)
+
+    first = (out_copy, one_ref, held1, s1, r1)
+    second = (out_copy, three_ref, held3, s3, r3)
+    third = (back_copy, held1, back3_ref, sb3, rb3)
+    fourth = (back_copy, held3, back1_ref, sb1, rb1)
+    start_all(*first)
+    own1 = pltpu.make_async_copy(one_ref.at[channels_of(me)], held1.at[:, rows_of(me), :], own.at[0])
+    own1.start()
+    own3 = pltpu.make_async_copy(three_ref.at[channels_of(me)], held3.at[:, rows_of(me), :], own.at[1])
+    own3.start()
+    start_all(*second)
+
+    own1.wait()
+    wait_all(*first)
+
+    def forward(c, carry):
+        spectrum = jnp.dot(b_ref[...], held1[c], preferred_element_type=f32)
+        spec[c] = spectrum
+        filtered = (spectrum * kern_ref[c].astype(f32)).astype(bf16)
+        held1[c] = jnp.dot(g_ref[...], filtered, preferred_element_type=f32).astype(bf16)
+        return carry
+
+    lax.fori_loop(0, wide, forward, 0)
+    start_all(*third)
+    keep3 = pltpu.make_async_copy(held1.at[:, rows_of(me), :], back3_ref.at[channels_of(me)], own.at[2])
+    keep3.start()
+    own3.wait()
+    wait_all(*second)
+
+    def backward(c, carry):
+        d_freq = jnp.dot(gt_ref[...], held3[c], preferred_element_type=f32)
+        gk_ref[c] = (d_freq * spec[c]).astype(bf16)
+        d_spec = (d_freq * kern_ref[c].astype(f32)).astype(bf16)
+        held3[c] = jnp.dot(bt_ref[...], d_spec, preferred_element_type=f32).astype(bf16)
+        return carry
+
+    lax.fori_loop(0, wide, backward, 0)
+    start_all(*fourth)
+    keep1 = pltpu.make_async_copy(held3.at[:, rows_of(me), :], back1_ref.at[channels_of(me)], own.at[3])
+    keep1.start()
+    keep3.wait()
+    wait_all(*third)
+    keep1.wait()
+    wait_all(*fourth)
+
+
+def exchange(one, three, kern, second_block, third_block, n):
+    dma = pltpu.SemaphoreType.DMA
+    vmem = pl.BlockSpec(memory_space=pltpu.VMEM)
+    hbm = pl.BlockSpec(memory_space=pl.ANY)
+    return pl.pallas_call(
+        functools.partial(exchange_kernel, n),
+        out_shape=(
+            jax.ShapeDtypeStruct(one.shape, bf16),
+            jax.ShapeDtypeStruct(three.shape, bf16),
+            jax.ShapeDtypeStruct(kern.shape, bf16),
+        ),
+        in_specs=[hbm, hbm] + [vmem] * 5,
+        out_specs=(hbm, hbm, vmem),
+        scratch_shapes=[
+            pltpu.VMEM(kern.shape, bf16),
+            pltpu.VMEM(kern.shape, bf16),
+            pltpu.VMEM(kern.shape, f32),
+        ] + [dma((n,))] * 8 + [dma((4,))],
+        compiler_params=pltpu.CompilerParams(collective_id=1, has_side_effects=True),
+        name="exchange",
+    )(one, three, kern, second_block, second_block.T, third_block, third_block.T)
 
 
 def on_device(tokens, w_value, w_gate, first_block, second_block, third_block, fourth_block, kernel, skip_gain, cotangent):
@@ -123,39 +241,19 @@
     value = jnp.dot(tokens, w_value, preferred_element_type=f32).astype(bf16)
     cube = value.reshape(rows_here, n2, d)
     section_one = jnp.einsum("abc,pb->cap", cube, first_block, preferred_element_type=f32).astype(bf16)
-    one_here = lax.all_to_all(section_one, "seq", split_axis=0, concat_axis=1, tiled=True)
-
     gate = jnp.dot(tokens, w_gate, preferred_element_type=f32).astype(bf16)
     upstream = cotangent.astype(f32)
     d_mix = (upstream * gate.astype(f32)).astype(bf16)
     d_mix_cube = d_mix.reshape(rows_here, n2, d)
     d_three = jnp.einsum("rsc,sp->crp", d_mix_cube, fourth_block, preferred_element_type=f32).astype(bf16)
     skip_term = jnp.sum(d_mix.astype(f32) * value.astype(f32), axis=0)
-    one_here, d_three, skip_term = lax.optimization_barrier((one_here, d_three, skip_term))
-    three_here = lax.all_to_all(d_three, "seq", split_axis=0, concat_axis=1, tiled=True)
-
-    spectrum = jnp.einsum("cap,qa->cqp", one_here, second_block, preferred_element_type=f32)
-    filtered = (spectrum * kernel.astype(f32)).astype(bf16)
-    section_three = jnp.einsum("cqp,rq->crp", filtered, third_block, preferred_element_type=f32).astype(bf16)
-    split_three = section_three.reshape(section_three.shape[0], n, rows_here, n2)
-    three_here, split_three, spectrum = lax.optimization_barrier((three_here, split_three, spectrum))
-    back_three = lax.all_to_all(split_three, "seq", split_axis=1, concat_axis=0, tiled=True)[:, 0]
-
-    d_freq = jnp.einsum("crp,rq->cqp", three_here, third_block, preferred_element_type=f32)
-    grad_kernel = (d_freq * spectrum).astype(bf16)
-    d_spec = (d_freq * kernel.astype(f32)).astype(bf16)
-    d_one = jnp.einsum("cqp,qa->cap", d_spec, second_block, preferred_element_type=f32).astype(bf16)
-    split_one = d_one.reshape(d_one.shape[0], n, rows_here, n2)
-    back_three, split_one, grad_kernel = lax.optimization_barrier((back_three, split_one, grad_kernel))
-    back_one = lax.all_to_all(split_one, "seq", split_axis=1, concat_axis=0, tiled=True)[:, 0]
-
+    back_three, back_one, grad_kernel = exchange(section_one, d_three, kernel, second_block, third_block, n)
     conv = jnp.einsum("crp,sp->rsc", back_three, fourth_block, preferred_element_type=f32)
     mixed = conv.reshape(local_rows, d) + skip_gain * value.astype(f32)
     d_gate = (upstream * mixed).astype(bf16)
     factor = 1.0 / jnp.sqrt(jnp.asarray(n1 * n2, f32))
     gate_term = (jnp.dot(tokens.T, d_gate, preferred_element_type=f32) * factor).astype(bf16)
     gate_grad = jnp.dot(d_gate, w_gate.T, preferred_element_type=f32)
-    back_one, gate_term, gate_grad = lax.optimization_barrier((back_one, gate_term, gate_grad))
 
     d_cube = jnp.einsum("cap,pb->abc", back_one, first_block, preferred_element_type=f32)
     d_value = (d_cube.reshape(local_rows, d) + skip_gain * d_mix.astype(f32)).astype(bf16)

time: 508 us -> 506 us (level); the launches traced: 500 us -> 505 us
  Pallas kernels: 48.4 us -> 414 us
  waiting for transfers between devices: 280 us -> 0 us
  starting transfers between devices: 39.2 us -> 0 us
  local copies, waits for them, and re-layouts: 44.8 us -> 23.3 us
  matrix products: 68.6 us -> 52.3 us
    pallas_call x0 -> x1, Pallas kernels: none -> 368 us  [exchange(): pl.pallas_call(functools.partial(exchange_kernel, n), out_shape=(jax.Shap...]
    all_to_all x4 -> x0, waiting for transfers between devices: 280 us -> none  [the longest x1 80.7 us: on_device(): lax.all_to_all(section_one, 'seq', split_axis=0, concat_axis=1, tiled=True)]
    all_to_all x4 -> x0, starting transfers between devices: 39.2 us -> none  [the longest x1 10.8 us: on_device(): lax.all_to_all(split_one, 'seq', split_axis=1, concat_axis=0, tiled=True)]
    dot_general x4 -> x0, matrix products: 18.5 us -> none  [the longest x1 8.1 us: on_device(): jnp.einsum('crp,rq->cqp', three_here, third_block, preferred_element_type...]
    reshape x0 -> x2, local copies, waits for them, and re-layouts: none -> 15.9 us  [the longest x1 7.98 us: on_device(): cube = value.reshape(rows_here, n2, d)]
    convert_element_type x2 -> x0, other arithmetic: 14.1 us -> none  [the longest x1 7.78 us: on_device(): d_gate = (upstream * mixed).astype(bf16)]
    unnamed x38 -> x27, local copies, waits for them, and re-layouts: 17.1 us -> 5.45 us
    optimization_barrier x3 -> x0, local copies, waits for them, and re-layouts: 11.5 us -> none  [the longest x1 4.59 us: on_device(): lax.optimization_barrier((back_three, split_one, grad_kernel))]
  transfers between devices with their start and end apart: 4 -> 0, of which waited for: 4 -> 0; matrix products, arithmetic and copies ran while one was open for 12% -> 0% of each run, Pallas kernels for 0% -> 0%
where the time goes in v2:
time: 506 us; the launch traced here: 505 us
  Pallas kernels  414 us (82%)
  matrix products  52.3 us (10%)
  local copies, waits for them, and re-layouts  23.3 us (5%)
  other arithmetic  14.7 us (3%)
    pallas_call x1, Pallas kernels, exchange(): pl.pallas_call(functools.partial(exchange_kernel, n), out_shape=(jax.Shap...  368 us
    pallas_call x1, Pallas kernels, all_sum(): pl.pallas_call(functools.partial(reduce_kernel, n), out_shape=(jax.ShapeD...  45.9 us
    reduce_sum x1, other arithmetic, on_device(): skip_term = jnp.sum(d_mix.astype(f32) * value.astype(f32), axis=0)  10.9 us

profile of v2, /device:TPU:25, one launch (start us, length us, event | category | flops | bytes accessed | tf_op | source)
XLA Modules:
  0.0 504.9 jit_solution(5126347431576941898)
XLA Ops:
  0.6 0.0 copy-start
  0.6 1.7 copy.18
  2.4 1.7 copy.19
  4.0 6.7 %convolution_convert_fusion.1 = bf16[4096,512]{1,0:T(8,128)(2,1)} fusion(bf16[4096,512]{1,0:T(8,128)(2,1)} %param.10, bf16[512,512]{1,0:T(8,128)(2,1)S(1)} %copy-done), kind=kOutput, calls=%fused_computation.13 | convolution fusion | flops 2149580800 | bytes 8912896 | tf_op jit(solution)/shard_map/dot_general | solution.py:241
  10.7 4.4 fusion
  15.2 8.0 %copy.25 = bf16[16,256,512]{1,0,2:T(8,128)(2,1)} copy(bf16[16,256,512]{2,1,0:T(8,128)(2,1)} %bitcast.52) | data formatting | bytes 8388608 | tf_op jit(solution)/shard_map/reshape | solution.py:247
  23.1 0.0 copy-done.7
  23.1 5.4 %convert_bitcast_fusion.three_ref = bf16[512,16,256]{2,1,0:T(8,128)(2,1)} fusion(bf16[16,256,512]{1,0,2:T(8,128)(2,1)} %copy.25, bf16[256,256]{1,0:T(8,128)(2,1)S(1)} %copy-done.7), kind=kOutput, calls=%fused_computation.18 | convolution fusion | flops 1075838976 | bytes 8519680 | tf_op jit(solution)/shard_map/rsc,sp->crp/dot_general | solution.py:248
  28.5 8.0 %copy.23 = bf16[16,256,512]{1,0,2:T(8,128)(2,1)} copy(bf16[16,256,512]{2,1,0:T(8,128)(2,1)} %bitcast.51) | data formatting | bytes 8388608 | tf_op jit(solution)/shard_map/reshape | solution.py:242
  36.5 5.4 %convert_bitcast_fusion.1.one_ref = bf16[512,16,256]{2,1,0:T(8,128)(2,1)} fusion(bf16[16,256,512]{1,0,2:T(8,128)(2,1)} %copy.23, bf16[256,256]{1,0:T(8,128)(2,1)S(1)} %copy-done.6), kind=kOutput, calls=%fused_computation.19 | convolution fusion | flops 1075838976 | bytes 8519680 | tf_op jit(solution)/shard_map/abc,pb->cap/dot_general | solution.py:243
  42.0 368.0 %exchange.1 = (bf16[512,16,256]{2,1,0:T(8,128)(2,1)}, bf16[512,16,256]{2,1,0:T(8,128)(2,1)}, bf16[32,256,256]{2,1,0:T(8,128)(2,1)}) custom-call(bf16[512,16,256]{2,1,0:T(8,128)(2,1)} %convert_bitcast_fusion.1.one_ref, bf16[512,16,256]{2,1,0:T(8,128)(2,1)} %convert_bitcast_fusion.three_ref, bf16[32,256,256]{2,1,0:T(8,128)(2,1)} %kern_ref.1, ...), custom_call_target="tpu_custom_call" | custom-call | tf_op jit(solution)/shard_map/exchange/pallas_call | solution.py:216
  410.0 8.8 %fusion.8 = f32[512,16,256]{0,2,1:T(8,128)} fusion(bf16[512,16,256]{2,1,0:T(8,128)(2,1)} %get-tuple-element.9, bf16[256,256]{1,0:T(8,128)(2,1)S(1)} %copy-done.6), kind=kOutput, calls=%fused_computation.16 | convolution fusion | flops 1073741824 | bytes 12713984 | tf_op jit(solution)/shard_map/cap,pb->abc/dot_general | solution.py:258
  418.8 3.1 fusion.6
  421.9 10.9 %fusion.5 = (f32[512]{0:T(512)S(1)}, bf16[4096,512]{1,0:T(8,128)(2,1)}, bf16[4096,512]{1,0:T(8,128)(2,1)S(1)}) fusion(bf16[4096,512]{1,0:T(8,128)(2,1)} %convolution_convert_fusion.1, bf16[4096,512]{1,0:T(8,128)(2,1)} %fusion, f32[512]{0:T(512)S(1)} %copy-done.9, f32[512,16,256]{0,2,1:T(8,128)} %fusion.8, f32[512,16,256]{0,2,1:T(8,128)S(1)} %fusion.6, ...), kind=kLoop, calls=%fused_computation.10 | loop fusion | flops 25165312 | bytes 37752832 | tf_op jit(solution)/shard_map/reduce_sum | solution.py:249
  432.7 0.6 pad.4.s_ref
  433.4 6.7 %fusion.13 = bf16[512,512]{1,0:T(8,128)(2,1)S(1)} fusion(bf16[4096,512]{1,0:T(8,128)(2,1)} %get-tuple-element.15, bf16[4096,512]{1,0:T(8,128)(2,1)} %param.10), kind=kOutput, calls=%fused_computation.25 | convolution fusion | flops 2148007936 | bytes 8912896 | tf_op jit(solution)/shard_map/dot_general | solution.py:261
  440.1 2.4 fusion.12
  442.5 1.0 pad_maximum_fusion.x_ref
  443.5 45.9 %all_sum.1 = (bf16[1024,512]{1,0:T(8,128)(2,1)}, f32[8,128]{1,0:T(8,128)}) custom-call(bf16[1024,512]{1,0:T(8,128)(2,1)} %pad_maximum_fusion.x_ref, f32[8,128]{1,0:T(8,128)} %pad.4.s_ref), custom_call_target="tpu_custom_call" | custom-call | tf_op jit(solution)/shard_map/all_sum/pallas_call | solution.py:112
  489.4 1.3 slice_bitcast_fusion
  490.7 2.8 convert.1
  493.5 4.9 fusion.18
  498.4 4.5 add_convert_fusion
  502.9 2.0 copy.36
  (23 shorter events, 0.0 us)
Async XLA Ops:
  0.6 3.4 copy-start
  4.0 6.7 %copy-start.4 = (bf16[4096,512]{1,0:T(8,128)(2,1)S(1)}, bf16[4096,512]{1,0:T(8,128)(2,1)}, u32[]{:S(2)}) copy-start(bf16[4096,512]{1,0:T(8,128)(2,1)} %param.19) | copy-start | bytes 12582916
  4.0 6.7 %copy-start.8 = (bf16[512,512]{1,0:T(8,128)(2,1)S(1)}, bf16[512,512]{1,0:T(8,128)(2,1)}, u32[]{:S(2)}) copy-start(bf16[512,512]{1,0:T(8,128)(2,1)} %param.12) | copy-start | bytes 1572868
  4.0 6.7 %copy-start.10 = (bf16[4096,512]{1,0:T(8,128)(2,1)S(1)}, bf16[4096,512]{1,0:T(8,128)(2,1)}, u32[]{:S(2)}) copy-start(bf16[4096,512]{1,0:T(8,128)(2,1)} %param.10) | copy-start | bytes 12582916
  15.2 8.0 %copy-start.7 = (bf16[256,256]{1,0:T(8,128)(2,1)S(1)}, bf16[256,256]{1,0:T(8,128)(2,1)}, u32[]{:S(2)}) copy-start(bf16[256,256]{1,0:T(8,128)(2,1)} %param.16) | copy-start | bytes 393220
  28.5 8.0 %copy-start.6 = (bf16[256,256]{1,0:T(8,128)(2,1)S(1)}, bf16[256,256]{1,0:T(8,128)(2,1)}, u32[]{:S(2)}) copy-start(bf16[256,256]{1,0:T(8,128)(2,1)} %param.13) | copy-start | bytes 393220
  410.0 8.8 %copy-start.3 = (bf16[512,16,256]{2,1,0:T(8,128)(2,1)S(1)}, bf16[512,16,256]{2,1,0:T(8,128)(2,1)}, u32[]{:S(2)}) copy-start(bf16[512,16,256]{2,1,0:T(8,128)(2,1)} %get-tuple-element.10) | copy-start | bytes 12582916
  418.8 3.1 copy-start.9
  432.7 7.3 %copy-start.1 = (bf16[4096,512]{1,0:T(8,128)(2,1)}, bf16[4096,512]{1,0:T(8,128)(2,1)S(1)}, u32[]{:S(2)}) copy-start(bf16[4096,512]{1,0:T(8,128)(2,1)S(1)} %get-tuple-element.16) | copy-start | bytes 12582916
  433.4 6.7 %copy-start.11 = (bf16[4096,512]{1,0:T(8,128)(2,1)S(1)}, bf16[4096,512]{1,0:T(8,128)(2,1)}, u32[]{:S(2)}) copy-start(bf16[4096,512]{1,0:T(8,128)(2,1)} %param.10) | copy-start | bytes 12582916
  493.5 4.9 copy-start.2
  498.4 4.5 copy-start.5

commit v3 on v2

--- a/solution.py
+++ b/solution.py
@@ -126,11 +126,25 @@
     )(x, s)
 
 
-def exchange_kernel(n, one_ref, three_ref, kern_ref, b_ref, bt_ref, g_ref, gt_ref, back3_ref, back1_ref, gk_ref,
-                    held1, held3, spec, s1, r1, s3, r3, sb3, rb3, sb1, rb1, own):
+def flip(x):
+    return x.astype(f32).T.astype(bf16)
+
+
+def dot(x, y, left, right):
+    return lax.dot_general(x, y, (((left,), (right,)), ((), ())), preferred_element_type=f32)
+
+
+def mixer_kernel(n, factor, tok_ref, cot_ref, kern_hbm, wv_ref, wg_ref, f_ref, b_ref, g_ref, h_ref, gain_ref,
+                 gtok_hbm, gk_hbm, back3_hbm, back1_hbm, terms_ref, skip_ref,
+                 value, d_mix, kern, one, three, held1, held3, work, spec, acc, ft, bt, gt,
+                 s1, r1, s3, r3, sb3, rb3, sb1, rb1, own, rows_sem):
     me = lax.axis_index("seq")
-    wide = kern_ref.shape[0]
-    rows = one_ref.shape[1]
+    wide = kern.shape[0]
+    total_rows = held1.shape[0]
+    rows = tok_ref.shape[0]
+    dim = tok_ref.shape[2]
+    load = pltpu.make_async_copy(kern_hbm, kern, own.at[4])
+    load.start()
     barrier = pltpu.get_barrier_semaphore()
 
     def greet(k, carry):
@@ -138,98 +152,162 @@
         return carry
 
     lax.fori_loop(1, n, greet, 0)
+
+    ft[...] = flip(f_ref[...])
+    bt[...] = flip(b_ref[...])
+    gt[...] = flip(g_ref[...])
+
+    def section_one(a, carry):
+        v = jnp.dot(tok_ref[a], wv_ref[...], preferred_element_type=f32).astype(bf16)
+        value[a] = v
+        one[a] = dot(v, ft[...], 0, 0).astype(bf16)
+        return carry
+
+    lax.fori_loop(0, rows, section_one, 0)
     pl.semaphore_wait(barrier, n - 1)
 
     def channels_of(d):
         return pl.ds(pl.multiple_of(d * wide, wide), wide)
 
     def rows_of(d):
-        return pl.ds(pl.multiple_of(d * rows, rows), rows)
+        return pl.ds(d * rows, rows)
 
     def out_copy(src, dst, send, recv, k):
         peer = lax.rem(me + k, n)
         return pltpu.make_async_remote_copy(
-            src_ref=src.at[channels_of(peer)], dst_ref=dst.at[:, rows_of(me), :], send_sem=send.at[k], recv_sem=recv.at[k],
+            src_ref=src.at[:, channels_of(peer), :], dst_ref=dst.at[rows_of(me)], send_sem=send.at[k], recv_sem=recv.at[k],
             device_id={"seq": peer}, device_id_type=MESH)
 
     def back_copy(src, dst, send, recv, k):
         peer = lax.rem(me + k, n)
         return pltpu.make_async_remote_copy(
-            src_ref=src.at[:, rows_of(peer), :], dst_ref=dst.at[channels_of(me)], send_sem=send.at[k], recv_sem=recv.at[k],
+            src_ref=src.at[rows_of(peer)], dst_ref=dst.at[:, channels_of(me), :], send_sem=send.at[k], recv_sem=recv.at[k],
             device_id={"seq": peer}, device_id_type=MESH)
 
     def start_all(copy, *refs):
-        lax.fori_loop(1, n, lambda k, c: (copy(*refs, k).start(), c)[1], 0)
+        def go(i, carry):
+            k = n // 2 + (2 * lax.rem(i, 2) - 1) * lax.div(i + 1, 2)
+            copy(*refs, k).start()
+            return carry
+
+        lax.fori_loop(0, n - 1, go, 0)
 
     def wait_all(copy, *refs):
         lax.fori_loop(1, n, lambda k, c: (copy(*refs, k).wait(), c)[1], 0)
 
-    first = (out_copy, one_ref, held1, s1, r1)
-    second = (out_copy, three_ref, held3, s3, r3)
-    third = (back_copy, held1, back3_ref, sb3, rb3)
-    fourth = (back_copy, held3, back1_ref, sb1, rb1)
+    first = (out_copy, one, held1, s1, r1)
+    second = (out_copy, three, held3, s3, r3)
+    third = (back_copy, held1, back3_hbm, sb3, rb3)
+    fourth = (back_copy, held3, back1_hbm, sb1, rb1)
     start_all(*first)
-    own1 = pltpu.make_async_copy(one_ref.at[channels_of(me)], held1.at[:, rows_of(me), :], own.at[0])
+    own1 = pltpu.make_async_copy(one.at[:, channels_of(me), :], held1.at[rows_of(me)], own.at[0])
     own1.start()
-    own3 = pltpu.make_async_copy(three_ref.at[channels_of(me)], held3.at[:, rows_of(me), :], own.at[1])
+
+    def section_three_back(a, total):
+        up = cot_ref[a].astype(f32)
+        gate = jnp.dot(tok_ref[a], wg_ref[...], preferred_element_type=f32).astype(bf16)
+        m = (up * gate.astype(f32)).astype(bf16)
+        d_mix[a] = m
+        three[a] = dot(m, h_ref[...], 0, 0).astype(bf16)
+        return total + jnp.sum(m.astype(f32) * value[a].astype(f32), axis=0, keepdims=True)
+
+    skip_ref[...] = lax.fori_loop(0, rows, section_three_back, jnp.zeros((1, dim), f32)) * factor
+    own3 = pltpu.make_async_copy(three.at[:, channels_of(me), :], held3.at[rows_of(me)], own.at[1])
     own3.start()
     start_all(*second)
 
+    def gather(src):
+        def step(i, carry):
+            at = pl.ds(pl.multiple_of(i * 16, 16), 16)
+            work[:, at, :] = jnp.swapaxes(src[at], 0, 1)
+            return carry
+
+        lax.fori_loop(0, total_rows // 16, step, 0)
+
+    def scatter(dst):
+        def step(i, carry):
+            at = pl.ds(pl.multiple_of(i * 16, 16), 16)
+            dst[at] = jnp.swapaxes(work[:, at, :], 0, 1)
+            return carry
+
+        lax.fori_loop(0, total_rows // 16, step, 0)
+
     own1.wait()
+    load.wait()
     wait_all(*first)
+    gather(held1)
 
     def forward(c, carry):
-        spectrum = jnp.dot(b_ref[...], held1[c], preferred_element_type=f32)
+        spectrum = jnp.dot(b_ref[...], work[c], preferred_element_type=f32)
         spec[c] = spectrum
-        filtered = (spectrum * kern_ref[c].astype(f32)).astype(bf16)
-        held1[c] = jnp.dot(g_ref[...], filtered, preferred_element_type=f32).astype(bf16)
+        filtered = (spectrum * kern[c].astype(f32)).astype(bf16)
+        work[c] = jnp.dot(g_ref[...], filtered, preferred_element_type=f32).astype(bf16)
         return carry
 
     lax.fori_loop(0, wide, forward, 0)
+    scatter(held1)
     start_all(*third)
-    keep3 = pltpu.make_async_copy(held1.at[:, rows_of(me), :], back3_ref.at[channels_of(me)], own.at[2])
+    keep3 = pltpu.make_async_copy(held1.at[rows_of(me)], back3_hbm.at[:, channels_of(me), :], own.at[2])
     keep3.start()
     own3.wait()
     wait_all(*second)
+    gather(held3)
 
     def backward(c, carry):
-        d_freq = jnp.dot(gt_ref[...], held3[c], preferred_element_type=f32)
-        gk_ref[c] = (d_freq * spec[c]).astype(bf16)
-        d_spec = (d_freq * kern_ref[c].astype(f32)).astype(bf16)
-        held3[c] = jnp.dot(bt_ref[...], d_spec, preferred_element_type=f32).astype(bf16)
+        d_freq = jnp.dot(gt[...], work[c], preferred_element_type=f32)
+        d_spec = (d_freq * kern[c].astype(f32)).astype(bf16)
+        kern[c] = (d_freq * spec[c]).astype(bf16)
+        work[c] = jnp.dot(bt[...], d_spec, preferred_element_type=f32).astype(bf16)
         return carry
 
     lax.fori_loop(0, wide, backward, 0)
+    scatter(held3)
     start_all(*fourth)
-    keep1 = pltpu.make_async_copy(held3.at[:, rows_of(me), :], back1_ref.at[channels_of(me)], own.at[3])
+    keep1 = pltpu.make_async_copy(held3.at[rows_of(me)], back1_hbm.at[:, channels_of(me), :], own.at[3])
     keep1.start()
+    store = pltpu.make_async_copy(kern, gk_hbm, own.at[5])
+    store.start()
+
     keep3.wait()
     wait_all(*third)
+    fetch3 = pltpu.make_async_copy(back3_hbm, one, own.at[6])
+    fetch3.start()
+    fetch3.wait()
+    acc[...] = jnp.zeros_like(acc)
+
+    def gate_part(r, carry):
+        conv = dot(h_ref[...], one[r], 1, 1)
+        mixed = conv + gain_ref[...] * value[r].astype(f32)
+        d_gate = (cot_ref[r].astype(f32) * mixed).astype(bf16)
+        value[r] = d_gate
+        acc[...] += dot(tok_ref[r], d_gate, 0, 0)
+        return carry
+
+    lax.fori_loop(0, rows, gate_part, 0)
+    terms_ref[pl.ds(dim, dim), :] = (acc[...] * factor).astype(bf16)
+    acc[...] = jnp.zeros_like(acc)
+
+    store.wait()
     keep1.wait()
     wait_all(*fourth)
-
-
-def exchange(one, three, kern, second_block, third_block, n):
-    dma = pltpu.SemaphoreType.DMA
-    vmem = pl.BlockSpec(memory_space=pltpu.VMEM)
-    hbm = pl.BlockSpec(memory_space=pl.ANY)
-    return pl.pallas_call(
-        functools.partial(exchange_kernel, n),
-        out_shape=(
-            jax.ShapeDtypeStruct(one.shape, bf16),
-            jax.ShapeDtypeStruct(three.shape, bf16),
-            jax.ShapeDtypeStruct(kern.shape, bf16),
-        ),
-        in_specs=[hbm, hbm] + [vmem] * 5,
-        out_specs=(hbm, hbm, vmem),
-        scratch_shapes=[
-            pltpu.VMEM(kern.shape, bf16),
-            pltpu.VMEM(kern.shape, bf16),
-            pltpu.VMEM(kern.shape, f32),
-        ] + [dma((n,))] * 8 + [dma((4,))],
-        compiler_params=pltpu.CompilerParams(collective_id=1, has_side_effects=True),
-        name="exchange",
-    )(one, three, kern, second_block, second_block.T, third_block, third_block.T)
+    fetch1 = pltpu.make_async_copy(back1_hbm, three, own.at[7])
+    fetch1.start()
+    fetch1.wait()
+
+    def row_copy(r):
+        return pltpu.make_async_copy(d_mix.at[r], gtok_hbm.at[r], rows_sem.at[r])
+
+    def value_part(r, carry):
+        cube = dot(ft[...], three[r], 1, 1)
+        d_value = (cube + gain_ref[...] * d_mix[r].astype(f32)).astype(bf16)
+        acc[...] += dot(tok_ref[r], d_value, 0, 0)
+        d_mix[r] = (dot(d_value, wv_ref[...], 1, 1) + dot(value[r], wg_ref[...], 1, 1)).astype(bf16)
+        row_copy(r).start()
+        return carry
+
+    lax.fori_loop(0, rows, value_part, 0)
+    terms_ref[pl.ds(0, dim), :] = (acc[...] * factor).astype(bf16)
+    lax.fori_loop(0, rows, lambda r, c: (row_copy(r).wait(), c)[1], 0)
 
 
 def on_device(tokens, w_value, w_gate, first_block, second_block, third_block, fourth_block, kernel, skip_gain, cotangent):
@@ -237,31 +315,47 @@
     n1 = second_block.shape[0]
     n2 = first_block.shape[0]
     local_rows, d = tokens.shape
-    rows_here = n1 // n
-    value = jnp.dot(tokens, w_value, preferred_element_type=f32).astype(bf16)
-    cube = value.reshape(rows_here, n2, d)
-    section_one = jnp.einsum("abc,pb->cap", cube, first_block, preferred_element_type=f32).astype(bf16)
-    gate = jnp.dot(tokens, w_gate, preferred_element_type=f32).astype(bf16)
-    upstream = cotangent.astype(f32)
-    d_mix = (upstream * gate.astype(f32)).astype(bf16)
-    d_mix_cube = d_mix.reshape(rows_here, n2, d)
-    d_three = jnp.einsum("rsc,sp->crp", d_mix_cube, fourth_block, preferred_element_type=f32).astype(bf16)
-    skip_term = jnp.sum(d_mix.astype(f32) * value.astype(f32), axis=0)
-    back_three, back_one, grad_kernel = exchange(section_one, d_three, kernel, second_block, third_block, n)
-    conv = jnp.einsum("crp,sp->rsc", back_three, fourth_block, preferred_element_type=f32)
-    mixed = conv.reshape(local_rows, d) + skip_gain * value.astype(f32)
-    d_gate = (upstream * mixed).astype(bf16)
-    factor = 1.0 / jnp.sqrt(jnp.asarray(n1 * n2, f32))
-    gate_term = (jnp.dot(tokens.T, d_gate, preferred_element_type=f32) * factor).astype(bf16)
-    gate_grad = jnp.dot(d_gate, w_gate.T, preferred_element_type=f32)
-
-    d_cube = jnp.einsum("cap,pb->abc", back_one, first_block, preferred_element_type=f32)
-    d_value = (d_cube.reshape(local_rows, d) + skip_gain * d_mix.astype(f32)).astype(bf16)
-    grad_tokens = (jnp.dot(d_value, w_value.T, preferred_element_type=f32) + gate_grad).astype(bf16)
-    value_term = (jnp.dot(tokens.T, d_value, preferred_element_type=f32) * factor).astype(bf16)
-    skip_rows = jnp.pad((skip_term * factor).reshape(-1, 128), ((0, 8 - d // 128), (0, 0)))
-    sums, skip_sum = all_sum(jnp.concatenate([value_term, gate_term]), skip_rows, n)
-    return (grad_tokens, grad_kernel, sums.astype(f32).reshape(2, d, d), skip_sum[: d // 128].reshape(d))
+    rows = n1 // n
+    wide = kernel.shape[0]
+    factor = float(n1 * n2) ** -0.5
+    dma = pltpu.SemaphoreType.DMA
+    vmem = pl.BlockSpec(memory_space=pltpu.VMEM)
+    hbm = pl.BlockSpec(memory_space=pl.ANY)
+    by_row = (rows, n2, d)
+    on_link = (rows, d, n2)
+    square = pltpu.VMEM((n1, n1), bf16)
+    grad_tokens, grad_kernel, _, _, terms, skip_term = pl.pallas_call(
+        functools.partial(mixer_kernel, n, factor),
+        out_shape=(
+            jax.ShapeDtypeStruct(by_row, bf16),
+            jax.ShapeDtypeStruct(kernel.shape, bf16),
+            jax.ShapeDtypeStruct(on_link, bf16),
+            jax.ShapeDtypeStruct(on_link, bf16),
+            jax.ShapeDtypeStruct((2 * d, d), bf16),
+            jax.ShapeDtypeStruct((1, d), f32),
+        ),
+        in_specs=[vmem, vmem, hbm] + [vmem] * 7,
+        out_specs=(hbm, hbm, hbm, hbm, vmem, vmem),
+        scratch_shapes=[
+            pltpu.VMEM(by_row, bf16),
+            pltpu.VMEM(by_row, bf16),
+            pltpu.VMEM(kernel.shape, bf16),
+            pltpu.VMEM(on_link, bf16),
+            pltpu.VMEM(on_link, bf16),
+            pltpu.VMEM((n1, wide, n2), bf16),
+            pltpu.VMEM((n1, wide, n2), bf16),
+            pltpu.VMEM((wide, n1, n2), bf16),
+            pltpu.VMEM((wide, n1, n2), f32),
+            pltpu.VMEM((d, d), f32),
+            pltpu.VMEM((n2, n2), bf16), square, square,
+        ] + [dma((n,))] * 8 + [dma((8,)), dma((rows,))],
+        compiler_params=pltpu.CompilerParams(collective_id=1, has_side_effects=True, vmem_limit_bytes=66_000_000),
+        name="mixer",
+    )(tokens.reshape(by_row), cotangent.reshape(by_row), kernel, w_value, w_gate, first_block, second_block,
+      third_block, fourth_block, skip_gain.reshape(1, d))
+    skip_rows = jnp.pad(skip_term.reshape(-1, 128), ((0, 8 - d // 128), (0, 0)))
+    sums, skip_sum = all_sum(terms, skip_rows, n)
+    return (grad_tokens.reshape(local_rows, d), grad_kernel, sums.astype(f32).reshape(2, d, d), skip_sum[: d // 128].reshape(d))
 
 
 def solution(mesh):

time: 506 us -> 444 us (0.88)
  matrix products: 52.3 us -> 0 us
  Pallas kernels: 414 us -> 430 us
  local copies, waits for them, and re-layouts: 23.3 us -> 9.16 us
  other arithmetic: 14.7 us -> 2.83 us
    dot_general x10 -> x0, matrix products: 52.3 us -> none  [the longest x1 8.81 us: on_device(): jnp.einsum('cap,pb->abc', back_one, first_block, preferred_element_type=f32)]
    pallas_call x1, Pallas kernels: 45.9 us -> 64.2 us  [all_sum(): pl.pallas_call(functools.partial(reduce_kernel, n), out_shape=(jax.ShapeD...]
    reshape x2 -> x0, local copies, waits for them, and re-layouts: 15.9 us -> none  [the longest x1 7.98 us: on_device(): cube = value.reshape(rows_here, n2, d)]
    reduce_sum x1 -> x0, other arithmetic: 10.9 us -> none  [on_device(): skip_term = jnp.sum(d_mix.astype(f32) * value.astype(f32), axis=0)]
where the time goes in v3:
time: 444 us; the launch traced here: 443 us
  Pallas kernels  430 us (97%)
  local copies, waits for them, and re-layouts  9.16 us (2%)
    pallas_call x1, Pallas kernels, on_device(): pl.pallas_call(functools.partial(mixer_kernel, n, factor), out_shape=(jax...  366 us
    pallas_call x1, Pallas kernels, all_sum(): pl.pallas_call(functools.partial(reduce_kernel, n), out_shape=(jax.ShapeD...  64.2 us

profile of v3, /device:TPU:25, one launch (start us, length us, event | category | flops | bytes accessed | tf_op | source)
XLA Modules:
  0.0 443.0 jit_solution(6923593385271193960)
XLA Ops:
  0.6 366.2 %mixer.1 = (bf16[16,256,512]{2,1,0:T(8,128)(2,1)}, bf16[32,256,256]{2,1,0:T(8,128)(2,1)}, bf16[16,512,256]{2,1,0:T(8,128)(2,1)}, bf16[16,512,256]{2,1,0:T(8,128)...) custom-call(bf16[16,256,512]{2,1,0:T(8,128)(2,1)} %bitcast.10, bf16[16,256,512]{2,1,0:T(8,128)(2,1)} %bitcast.11, ...), custom_call_target="tpu_custom_call" | custom-call | tf_op jit(solution)/shard_map/mixer/pallas_call | solution.py:327
  366.8 1.3 pad.4.s_ref
  368.1 64.2 %all_sum.1 = (bf16[1024,512]{1,0:T(8,128)(2,1)}, f32[8,128]{1,0:T(8,128)}) custom-call(bf16[1024,512]{1,0:T(8,128)(2,1)} %get-tuple-element.12.x_ref, f32[8,128]{1,0:T(8,128)} %pad.4.s_ref), custom_call_target="tpu_custom_call" | custom-call | tf_op jit(solution)/shard_map/all_sum/pallas_call | solution.py:112
  432.3 1.3 slice_bitcast_fusion
  433.6 2.8 convert.1
  436.4 0.0 copy-start
  436.4 4.6 %copy.16 = bf16[4096,512]{1,0:T(8,128)(2,1)} copy(bf16[4096,512]{1,0:T(8,128)(2,1)} %bitcast.9) | data formatting | bytes 8388608
  441.0 0.0 copy-done
  441.0 2.0 copy.17
Async XLA Ops:
  436.4 4.6 %copy-start = (bf16[32,256,256]{2,1,0:T(8,128)(2,1)S(1)}, bf16[32,256,256]{2,1,0:T(8,128)(2,1)}, u32[]{:S(2)}) copy-start(bf16[32,256,256]{2,1,0:T(8,128)(2,1)} %get-tuple-element.21) | copy-start | bytes 12582916

commit v4 on v3

--- a/solution.py
+++ b/solution.py
@@ -8,6 +8,7 @@
 from jax.sharding import PartitionSpec as P
 
 MESH = pl.DeviceIdType.MESH
+PIECES = 4
 f32 = jnp.float32
 bf16 = jnp.bfloat16
 
@@ -157,15 +158,6 @@
     bt[...] = flip(b_ref[...])
     gt[...] = flip(g_ref[...])
 
-    def section_one(a, carry):
-        v = jnp.dot(tok_ref[a], wv_ref[...], preferred_element_type=f32).astype(bf16)
-        value[a] = v
-        one[a] = dot(v, ft[...], 0, 0).astype(bf16)
-        return carry
-
-    lax.fori_loop(0, rows, section_one, 0)
-    pl.semaphore_wait(barrier, n - 1)
-
     def channels_of(d):
         return pl.ds(pl.multiple_of(d * wide, wide), wide)
 
@@ -195,11 +187,42 @@
     def wait_all(copy, *refs):
         lax.fori_loop(1, n, lambda k, c: (copy(*refs, k).wait(), c)[1], 0)
 
-    first = (out_copy, one, held1, s1, r1)
+    slab = rows // PIECES
+
+    def first_piece(h):
+        def copy(k):
+            peer = lax.rem(me + k, n)
+            return pltpu.make_async_remote_copy(
+                src_ref=one.at[pl.ds(h * slab, slab), channels_of(peer), :],
+                dst_ref=held1.at[pl.ds(me * rows + h * slab, slab)],
+                send_sem=s1.at[h * n + k], recv_sem=r1.at[h * n + k],
+                device_id={"seq": peer}, device_id_type=MESH)
+
+        return copy
+
+    def fourth_piece(h):
+        def copy(k):
+            peer = lax.rem(me + k, n)
+            return pltpu.make_async_remote_copy(
+                src_ref=held3.at[pl.ds(peer * rows + h * slab, slab)],
+                dst_ref=back1_hbm.at[pl.ds(h * slab, slab), channels_of(me), :],
+                send_sem=sb1.at[h * n + k], recv_sem=rb1.at[h * n + k],
+                device_id={"seq": peer}, device_id_type=MESH)
+
+        return copy
+
     second = (out_copy, three, held3, s3, r3)
     third = (back_copy, held1, back3_hbm, sb3, rb3)
-    fourth = (back_copy, held3, back1_hbm, sb1, rb1)
-    start_all(*first)
+    def section_one(a, carry):
+        v = jnp.dot(tok_ref[a], wv_ref[...], preferred_element_type=f32).astype(bf16)
+        value[a] = v
+        one[a] = dot(v, ft[...], 0, 0).astype(bf16)
+        return carry
+
+    pl.semaphore_wait(barrier, n - 1)
+    for h in range(PIECES):
+        lax.fori_loop(h * slab, (h + 1) * slab, section_one, 0)
+        start_all(first_piece(h))
     own1 = pltpu.make_async_copy(one.at[:, channels_of(me), :], held1.at[rows_of(me)], own.at[0])
     own1.start()
 
@@ -234,7 +257,8 @@
 
     own1.wait()
     load.wait()
-    wait_all(*first)
+    for h in range(PIECES):
+        wait_all(first_piece(h))
     gather(held1)
 
     def forward(c, carry):
@@ -262,7 +286,8 @@
 
     lax.fori_loop(0, wide, backward, 0)
     scatter(held3)
-    start_all(*fourth)
+    for h in range(PIECES):
+        start_all(fourth_piece(h))
     keep1 = pltpu.make_async_copy(held3.at[rows_of(me)], back1_hbm.at[:, channels_of(me), :], own.at[3])
     keep1.start()
     store = pltpu.make_async_copy(kern, gk_hbm, own.at[5])
@@ -289,10 +314,6 @@
 
     store.wait()
     keep1.wait()
-    wait_all(*fourth)
-    fetch1 = pltpu.make_async_copy(back1_hbm, three, own.at[7])
-    fetch1.start()
-    fetch1.wait()
 
     def row_copy(r):
         return pltpu.make_async_copy(d_mix.at[r], gtok_hbm.at[r], rows_sem.at[r])
@@ -305,7 +326,13 @@
         row_copy(r).start()
         return carry
 
-    lax.fori_loop(0, rows, value_part, 0)
+    for h in range(PIECES):
+        wait_all(fourth_piece(h))
+        at = pl.ds(h * slab, slab)
+        fetch1 = pltpu.make_async_copy(back1_hbm.at[at], three.at[at], own.at[7])
+        fetch1.start()
+        fetch1.wait()
+        lax.fori_loop(h * slab, (h + 1) * slab, value_part, 0)
     terms_ref[pl.ds(0, dim), :] = (acc[...] * factor).astype(bf16)
     lax.fori_loop(0, rows, lambda r, c: (row_copy(r).wait(), c)[1], 0)
 
@@ -348,7 +375,7 @@
             pltpu.VMEM((wide, n1, n2), f32),
             pltpu.VMEM((d, d), f32),
             pltpu.VMEM((n2, n2), bf16), square, square,
-        ] + [dma((n,))] * 8 + [dma((8,)), dma((rows,))],
+        ] + [dma((PIECES * n,))] * 2 + [dma((n,))] * 4 + [dma((PIECES * n,))] * 2 + [dma((8,)), dma((rows,))],
         compiler_params=pltpu.CompilerParams(collective_id=1, has_side_effects=True, vmem_limit_bytes=66_000_000),
         name="mixer",
     )(tokens.reshape(by_row), cotangent.reshape(by_row), kernel, w_value, w_gate, first_block, second_block,

time: 444 us -> 428 us (0.964)
  Pallas kernels: 430 us -> 415 us
    pallas_call x1, Pallas kernels: 64.2 us -> 39.7 us  [all_sum(): pl.pallas_call(functools.partial(reduce_kernel, n), out_shape=(jax.ShapeD...]
    pallas_call x1, Pallas kernels: 366 us -> 375 us  [on_device(): pl.pallas_call(functools.partial(mixer_kernel, n, factor), out_shape=(jax...]
where the time goes in v4:
time: 428 us
  Pallas kernels  415 us (97%)
  local copies, waits for them, and re-layouts  9.16 us (2%)
    pallas_call x1, Pallas kernels, on_device(): pl.pallas_call(functools.partial(mixer_kernel, n, factor), out_shape=(jax...  375 us
    pallas_call x1, Pallas kernels, all_sum(): pl.pallas_call(functools.partial(reduce_kernel, n), out_shape=(jax.ShapeD...  39.7 us

profile of v4, /device:TPU:25, one launch (start us, length us, event | category | flops | bytes accessed | tf_op | source)
XLA Modules:
  0.0 427.5 jit_solution(15820757893326581058)
XLA Ops:
  0.6 375.2 %mixer.1 = (bf16[16,256,512]{2,1,0:T(8,128)(2,1)}, bf16[32,256,256]{2,1,0:T(8,128)(2,1)}, bf16[16,512,256]{2,1,0:T(8,128)(2,1)}, bf16[16,512,256]{2,1,0:T(8,128)...) custom-call(bf16[16,256,512]{2,1,0:T(8,128)(2,1)} %bitcast.10, bf16[16,256,512]{2,1,0:T(8,128)(2,1)} %bitcast.11, ...), custom_call_target="tpu_custom_call" | custom-call | tf_op jit(solution)/shard_map/mixer/pallas_call | solution.py:354
  375.8 1.3 pad.4.s_ref
  377.1 39.7 %all_sum.1 = (bf16[1024,512]{1,0:T(8,128)(2,1)}, f32[8,128]{1,0:T(8,128)}) custom-call(bf16[1024,512]{1,0:T(8,128)(2,1)} %get-tuple-element.12.x_ref, f32[8,128]{1,0:T(8,128)} %pad.4.s_ref), custom_call_target="tpu_custom_call" | custom-call | tf_op jit(solution)/shard_map/all_sum/pallas_call | solution.py:113
  416.8 1.3 slice_bitcast_fusion
  418.0 2.8 convert.1
  420.9 0.0 copy-start
  420.9 4.6 %copy.16 = bf16[4096,512]{1,0:T(8,128)(2,1)} copy(bf16[4096,512]{1,0:T(8,128)(2,1)} %bitcast.9) | data formatting | bytes 8388608
  425.5 0.0 copy-done
  425.5 2.0 copy.17
Async XLA Ops:
  420.9 4.6 %copy-start = (bf16[32,256,256]{2,1,0:T(8,128)(2,1)S(1)}, bf16[32,256,256]{2,1,0:T(8,128)(2,1)}, u32[]{:S(2)}) copy-start(bf16[32,256,256]{2,1,0:T(8,128)(2,1)} %get-tuple-element.21) | copy-start | bytes 12582916
